TPU v7x, 256 devices: a whole 4x4x8 slice. The times are simulated.
256 devices in a mesh: slab: 16 (over y, x_hi, core), grp: 16 (over x_lo, z).
Axes of the slice: x: 4 (x_hi: 2, x_lo: 2; x = x_hi * 2 + x_lo), y: 4, z: 8, core: 2. Of those that a mesh axis runs over, the one named last changes fastest.
Arguments:
- cloud_states: float32 [2, 64, 4, 128, 1024], P(None, 'grp', None, 'slab'), may hold values from -6 to 6
- cloud_shift: int32 [2], replicated, may hold values from 9 to 15, as said below
- boost_wave: int32 [2], replicated, may hold values from -6 to 6, as said below
Outputs:
- evolved: float32 [2, 64, 4, 128, 1024], P(None, 'grp', None, 'slab')
Inputs may be any that keep to these rules, and one draw needn't show every extreme that they name: `cloud_shift`: one of the two entries equals 15. `boost_wave`: the first entry is 6; the second is negative.
All inputs are finite; a program needn't handle non-finite values.
Results may differ from a plain program's by a relative error of at most 0.00002.
Values sent between devices are 32-bit elements; how exact they have to be, the bound alone decides.
A program may use at most 64 MiB of HBM per device.

v0:
```python
import math

import jax
import jax.numpy as jnp
from jax import lax
from jax.sharding import PartitionSpec as P

NY = 32


stencil = (-49.0 / 18.0, 1.5, -0.15, 1.0 / 90.0)
coupling = 3.0
xi_factor = 1.2
chemical = 1.0
time_step = 0.1


def padded_2(x, sides, width):
    for axis, dim in sides:
        peers, length = (lax.axis_size(axis), x.shape[dim])
        up = [(i, (i + 1) % peers) for i in range(peers)]
        down = [(j, i) for i, j in up]
        last = lax.slice_in_dim(x, length - width, length, axis=dim)
        initial = lax.slice_in_dim(x, 0, width, axis=dim)
        before = lax.ppermute(last, axis, up)
        after = lax.ppermute(initial, axis, down)
        x = jnp.concatenate([before, x, after], axis=dim)
    return x


def shifted(x, axis, by):
    peers = lax.axis_size(axis)
    return lax.ppermute(x, axis, [(i, (i + by) % peers) for i in range(peers)])


def transverse(volume, row_width):
    cell_count = volume.shape[-1]
    column = lax.broadcasted_iota(jnp.int32, (cell_count,), 0) % row_width
    pad_spec = [(0, 0)] * (volume.ndim - 1) + [(3 * row_width, 3 * row_width)]
    padded = jnp.pad(volume, pad_spec)
    running = 2.0 * stencil[0] * volume
    base = 3 * row_width
    for offset in range(1, 4):
        for signed in (offset, -offset):
            across_rows = padded[
                ..., base + signed * row_width : base + signed * row_width + cell_count
            ]
            across_columns = padded[..., base + signed : base + signed + cell_count]
            inside = ((column + signed >= 0) & (column + signed < row_width)).astype(jnp.float32)
            running = running + stencil[offset] * (across_rows + across_columns * inside)
    return running


def along_depth(extended, planes):
    running = stencil[0] * extended[..., 3 : 3 + planes, :]
    for offset in range(1, 4):
        for signed in (offset, -offset):
            running = running + stencil[offset] * extended[..., 3 + signed : 3 + signed + planes, :]
    return running


def fields_of(totals):
    potential = xi_factor * jnp.square(jnp.cbrt(totals[0])) - chemical
    return jnp.stack([potential, -coupling * totals[1], -coupling * totals[2]])


def local_terms(states):
    particle_real = states[:, :, 0]
    particle_imag = states[:, :, 1]
    hole_real = states[:, :, 2]
    hole_imag = states[:, :, 3]
    density = jnp.sum(hole_real * hole_real + hole_imag * hole_imag, axis=(0, 1))
    pair_real = jnp.sum(particle_real * hole_real + particle_imag * hole_imag, axis=(0, 1))
    pair_imag = jnp.sum(particle_imag * hole_real - particle_real * hole_imag, axis=(0, 1))
    return jnp.stack([density, pair_real, pair_imag])


def potentials(states, total_states):
    partial_value = local_terms(states)
    totals = lax.psum(partial_value, "grp") / total_states
    return fields_of(totals)


def hamiltonian(states, fields):
    planes = states.shape[3]
    extended = padded_2(states, (("slab", 3),), 3)
    kinetic = -0.5 * (along_depth(extended, planes) + transverse(states, NY))
    potential = fields[0]
    gap_real = fields[1]
    gap_imag = fields[2]
    particle_real = states[:, :, 0]
    particle_imag = states[:, :, 1]
    hole_real = states[:, :, 2]
    hole_imag = states[:, :, 3]
    out_pr = (
        kinetic[:, :, 0] + potential * particle_real + gap_real * hole_real - gap_imag * hole_imag
    )
    out_pi = (
        kinetic[:, :, 1] + potential * particle_imag + gap_real * hole_imag + gap_imag * hole_real
    )
    out_hr = (
        gap_real * particle_real
        + gap_imag * particle_imag
        - kinetic[:, :, 2]
        - potential * hole_real
    )
    out_hi = (
        gap_real * particle_imag
        - gap_imag * particle_real
        - kinetic[:, :, 3]
        - potential * hole_imag
    )
    return jnp.stack([out_pr, out_pi, out_hr, out_hi], axis=2)


def advance(states, change, factor):
    return jnp.stack(
        [
            states[:, :, 0] + factor * change[:, :, 1],
            states[:, :, 1] - factor * change[:, :, 0],
            states[:, :, 2] + factor * change[:, :, 3],
            states[:, :, 3] - factor * change[:, :, 2],
        ],
        axis=2,
    )


def local(cloud_states, cloud_shift, boost_wave):
    slab_count = lax.axis_size("slab")
    slab_index = lax.axis_index("slab")
    _, per_group, _, planes, cell_count = cloud_states.shape
    total_states = per_group * lax.axis_size("grp")
    depth = planes * slab_count
    first_source = cloud_states[0]
    second_source = cloud_states[1]
    upper_one = shifted(first_source, "slab", 1)
    upper_two = shifted(first_source, "slab", 2)
    lower_one = shifted(second_source, "slab", -1)
    lower_two = shifted(second_source, "slab", -2)
    first_blocks = jnp.concatenate([upper_two, upper_one, first_source], axis=2)
    first_cloud = lax.dynamic_slice_in_dim(first_blocks, 2 * planes - cloud_shift[0], planes, 2)
    second_blocks = jnp.concatenate([second_source, lower_one, lower_two], axis=2)
    second_cloud = lax.dynamic_slice_in_dim(second_blocks, cloud_shift[1], planes, 2)
    placed = jnp.stack([first_cloud, second_cloud])
    global_plane = slab_index * planes + lax.broadcasted_iota(jnp.int32, (planes,), 0)
    phase_index = jnp.mod(boost_wave[:, None] * global_plane[None, :], depth)
    phases = 2.0 * math.pi / depth * phase_index.astype(jnp.float32)
    cosine_table = jnp.cos(phases)[:, None, :, None]
    sine_table = jnp.sin(phases)[:, None, :, None]
    particle_real = placed[:, :, 0]
    particle_imag = placed[:, :, 1]
    hole_real = placed[:, :, 2]
    hole_imag = placed[:, :, 3]
    boosted = jnp.stack(
        [
            particle_real * cosine_table - particle_imag * sine_table,
            particle_real * sine_table + particle_imag * cosine_table,
            hole_real * cosine_table + hole_imag * sine_table,
            hole_imag * cosine_table - hole_real * sine_table,
        ],
        axis=2,
    )
    change_now = hamiltonian(boosted, potentials(boosted, total_states))
    predicted = advance(boosted, change_now, time_step)
    change_next = hamiltonian(predicted, potentials(predicted, total_states))
    return advance(boosted, change_now + change_next, time_step / 2.0)


def solution(mesh):
    in_specs = (P(None, "grp", None, "slab", None), P(), P())
    out_specs = P(None, "grp", None, "slab", None)
    return jax.shard_map(local, mesh=mesh, in_specs=in_specs, out_specs=out_specs, check_vma=False)
```

profile of v0, /device:TPU:2, one launch (start us, length us, event | category | flops | bytes accessed | tf_op | source)
XLA Modules:
  0.0 331.5 jit_solution(14750241666101791552)
XLA Ops:
  6.5 1.3 slice_bitcast_fusion.1
  8.0 2.2 collective-permute-start
  10.2 3.5 %collective-permute-start.3 = (f32[4,4,8,1024]{3,2,1,0:T(8,128)S(1)}, f32[4,4,8,1024]{3,2,1,0:T(8,128)S(1)}, u32[]{:S(2)}, u32[]{:S(2)}) collective-permute-start(f32[4,4,8,1024]{3,2,1,0:T(8,128)S(1)} %get-tuple-element.53), channel_id=1, source_target_pairs={{0,224},{16,240},{32,0},{48,16},{64,32},{80,48},{96,64},{112,80},{... | collective-permute-start | bytes 1572872 | tf_op jit(solution)/shard_map/ppermute | solution.py:33
  13.7 2.6 collective-permute-start.2
  16.3 0.7 fusion.168
  20.5 4.7 %collective-permute-done.1 = f32[4,4,8,1024]{3,2,1,0:T(8,128)S(1)} collective-permute-done((f32[4,4,8,1024]{3,2,1,0:T(8,128)S(1)}, f32[4,4,8,1024]{3,2,1,0:T(8,128)S(1)}, u32[]{:S(2)}, u32[]{:S(2)}) %collective-permute-start.1) | collective-permute-done | bytes 524320 | tf_op jit(solution)/shard_map/ppermute | solution.py:33
  25.2 1.2 collective-permute-done
  26.4 0.2 copy_bitcast_fusion.1
  26.6 9.9 %collective-permute-done.3 = f32[4,4,8,1024]{3,2,1,0:T(8,128)S(1)} collective-permute-done((f32[4,4,8,1024]{3,2,1,0:T(8,128)S(1)}, f32[4,4,8,1024]{3,2,1,0:T(8,128)S(1)}, u32[]{:S(2)}, u32[]{:S(2)}) %collective-permute-start.3) | collective-permute-done | bytes 524320 | tf_op jit(solution)/shard_map/ppermute | solution.py:33
  36.5 7.7 %collective-permute-done.2 = f32[4,4,8,1024]{3,2,1,0:T(8,128)S(1)} collective-permute-done((f32[4,4,8,1024]{3,2,1,0:T(8,128)S(1)}, f32[4,4,8,1024]{3,2,1,0:T(8,128)S(1)}, u32[]{:S(2)}, u32[]{:S(2)}) %collective-permute-start.2) | collective-permute-done | bytes 524320 | tf_op jit(solution)/shard_map/ppermute | solution.py:33
  44.3 0.2 copy_bitcast_fusion
  44.5 1.2 add_reduce_fusion.2
  46.1 0.6 pad_maximum_fusion.7
  46.9 1.2 fusion.167
  48.1 5.5 %collective-permute-start.4 = (f32[2,4,4,3,1024]{4,3,1,0,2:T(4,128)}, f32[2,4,4,3,1024]{4,3,1,0,2:T(4,128)S(1)}, u32[]{:S(2)}, u32[]{:S(2)}) collective-permute-start(f32[2,4,4,3,1024]{4,3,1,0,2:T(4,128)} %get-tuple-element.50), channel_id=1, source_target_pairs={{16,0},{32,16},{48,32},{64,48},{80,64},{96,80},{112,96},{128,112},... | collective-permute-start | bytes 1179656 | tf_op jit(solution)/shard_map/ppermute | solution.py:26
  53.6 126.9 %all-reduce.5.cloned.1.call-done = f32[3,8,1024]{2,1,0:T(8,128)} async-done(((f32[3,8,1024]{2,1,0:T(8,128)}), f32[3,8,1024]{2,1,0:T(8,128)}) %all-reduce.5.cloned.1.call-update) | async-done | bytes 98320 | tf_op jit(solution)/shard_map/psum | solution.py:80
  180.5 0.9 broadcast_multiply_fusion.1
  181.5 0.5 pad_maximum_fusion
  182.1 3.4 %copy_multiply_fusion.1 = f32[2,4,4,8,1024]{4,3,2,1,0:T(8,128)S(1)} fusion(f32[2,4,4,8,1024]{4,3,1,0,2:T(8,128)S(1)} %pad_maximum_fusion.2, f32[2,4,4,11,1024]{4,3,1,0,2:T(8,128)S(1)} %get-tuple-element.49, f32[2,4,4,11,1024]{4,3,1,0,2:T(8,128)S(1)} %get-tuple-element.48, f32[1024]{0:T(1024)S(1)} %get-tuple-element.68, f32[1024]{0:T(1024)S(1)} %get-tuple-element.69, ...), kind=kLoop, calls=%fused_computation.120 | loop fusion | flops 10485760 | bytes 8413184 | tf_op jit(solution)/shard_map/mul | solution.py:87
  185.5 1.2 bitcast_add_fusion.5
  186.8 0.3 fusion.99
  187.2 0.7 pad_maximum_fusion.8
  188.0 1.3 fusion.166
  189.3 0.5 collective-permute-start.7
  189.8 126.2 %all-reduce.7.cloned.1.call-done = f32[3,8,1024]{2,1,0:T(8,128)} async-done(((f32[3,8,1024]{2,1,0:T(8,128)}), f32[3,8,1024]{2,1,0:T(8,128)}) %all-reduce.7.cloned.1.call-update) | async-done | bytes 98320 | tf_op jit(solution)/shard_map/psum | solution.py:80
  316.0 0.9 broadcast_multiply_fusion
  316.9 1.8 pad_maximum_fusion.1
  318.7 3.4 %copy_multiply_fusion = f32[2,4,4,8,1024]{4,3,2,1,0:T(8,128)S(1)} fusion(f32[2,4,4,8,1024]{4,3,1,0,2:T(8,128)S(1)} %pad_maximum_fusion.4, f32[2,4,4,11,1024]{4,3,1,0,2:T(8,128)S(1)} %get-tuple-element.45, f32[2,4,4,11,1024]{4,3,1,0,2:T(8,128)S(1)} %get-tuple-element.44, f32[1024]{0:T(1024)S(1)} %get-tuple-element.68, f32[1024]{0:T(1024)S(1)} %get-tuple-element.69, ...), kind=kLoop, calls=%fused_computation.119 | loop fusion | flops 10485760 | bytes 8413184 | tf_op jit(solution)/shard_map/mul | solution.py:87
  322.2 0.2 fusion.80
  322.4 0.7 copy-done
  323.3 0.2 maximum_add_fusion
  323.6 1.1 pad_maximum_fusion.5
  (42 shorter events, 1.4 us)
Async XLA Ops:
  6.5 9.8 %copy-start.7 = (s32[2]{0:T(128)S(1)}, s32[2]{0:T(128)}, u32[]{:S(2)}) copy-start(s32[2]{0:T(128)} %param.4) | copy-start | bytes 28
  6.5 13.8 %copy-start.8 = (s32[2]{0:T(128)S(1)}, s32[2]{0:T(128)}, u32[]{:S(2)}) copy-start(s32[2]{0:T(128)} %param.5) | copy-start | bytes 28
  6.5 174.0 %all-reduce.5.cloned.1.call-start = ((), (), s32[]{:S(2)}) async-start(), calls=%async_computation | async-start | bytes 196608 | tf_op jit(solution)/shard_map/psum | solution.py:80
  7.9 17.3 %collective-permute-start.1 = (f32[4,4,8,1024]{3,2,1,0:T(8,128)S(1)}, f32[4,4,8,1024]{3,2,1,0:T(8,128)S(1)}, u32[]{:S(2)}, u32[]{:S(2)}) collective-permute-start(f32[4,4,8,1024]{3,2,1,0:T(8,128)S(1)} %get-tuple-element.52), channel_id=1, source_target_pairs={{0,16},{16,32},{32,48},{48,64},{64,80},{80,96},{96,112},{112,128},... | collective-permute-start | bytes 1572872 | tf_op jit(solution)/shard_map/ppermute | solution.py:33
  8.0 18.4 %collective-permute-start = (f32[4,4,8,1024]{3,2,1,0:T(8,128)S(1)}, f32[4,4,8,1024]{3,2,1,0:T(8,128)S(1)}, u32[]{:S(2)}, u32[]{:S(2)}) collective-permute-start(f32[4,4,8,1024]{3,2,1,0:T(8,128)S(1)} %get-tuple-element.52), channel_id=1, source_target_pairs={{0,32},{16,48},{32,64},{48,80},{64,96},{80,112},{96,128},{112,144}... | collective-permute-start | bytes 1572872 | tf_op jit(solution)/shard_map/ppermute | solution.py:33
  10.2 26.4 %collective-permute-start.3 = (f32[4,4,8,1024]{3,2,1,0:T(8,128)S(1)}, f32[4,4,8,1024]{3,2,1,0:T(8,128)S(1)}, u32[]{:S(2)}, u32[]{:S(2)}) collective-permute-start(f32[4,4,8,1024]{3,2,1,0:T(8,128)S(1)} %get-tuple-element.53), channel_id=1, source_target_pairs={{0,224},{16,240},{32,0},{48,16},{64,32},{80,48},{96,64},{112,80},{... | collective-permute-start | bytes 1572872 | tf_op jit(solution)/shard_map/ppermute | solution.py:33
  13.7 30.6 %collective-permute-start.2 = (f32[4,4,8,1024]{3,2,1,0:T(8,128)S(1)}, f32[4,4,8,1024]{3,2,1,0:T(8,128)S(1)}, u32[]{:S(2)}, u32[]{:S(2)}) collective-permute-start(f32[4,4,8,1024]{3,2,1,0:T(8,128)S(1)} %get-tuple-element.53), channel_id=1, source_target_pairs={{0,240},{16,0},{32,16},{48,32},{64,48},{80,64},{96,80},{112,96},{1... | collective-permute-start | bytes 1572872 | tf_op jit(solution)/shard_map/ppermute | solution.py:33
  46.7 269.2 %all-reduce.7.cloned.1.call-start = ((), (), s32[]{:S(2)}) async-start(), calls=%async_computation.1 | async-start | bytes 196608 | tf_op jit(solution)/shard_map/psum | solution.py:80
  48.1 133.4 %collective-permute-start.4 = (f32[2,4,4,3,1024]{4,3,1,0,2:T(4,128)}, f32[2,4,4,3,1024]{4,3,1,0,2:T(4,128)S(1)}, u32[]{:S(2)}, u32[]{:S(2)}) collective-permute-start(f32[2,4,4,3,1024]{4,3,1,0,2:T(4,128)} %get-tuple-element.50), channel_id=1, source_target_pairs={{16,0},{32,16},{48,32},{64,48},{80,64},{96,80},{112,96},{128,112},... | collective-permute-start | bytes 1179656 | tf_op jit(solution)/shard_map/ppermute | solution.py:26
  53.6 127.9 %collective-permute-start.5 = (f32[2,4,4,3,1024]{4,3,1,0,2:T(4,128)}, f32[2,4,4,3,1024]{4,3,1,0,2:T(4,128)S(1)}, u32[]{:S(2)}, u32[]{:S(2)}) collective-permute-start(f32[2,4,4,3,1024]{4,3,1,0,2:T(4,128)} %get-tuple-element.51), channel_id=1, source_target_pairs={{0,16},{16,32},{32,48},{48,64},{64,80},{80,96},{96,112},{112,128},... | collective-permute-start | bytes 1179656 | tf_op jit(solution)/shard_map/ppermute | solution.py:25
  185.5 1.2 copy-start.3
  185.5 1.2 copy-start.4
  185.5 1.2 copy-start.5
  185.5 1.3 copy-start.6
  189.3 127.6 %collective-permute-start.6 = (f32[2,4,4,3,1024]{4,3,1,0,2:T(4,128)}, f32[2,4,4,3,1024]{4,3,1,0,2:T(4,128)}, u32[]{:S(2)}, u32[]{:S(2)}) collective-permute-start(f32[2,4,4,3,1024]{4,3,1,0,2:T(4,128)} %get-tuple-element.46), channel_id=1, source_target_pairs={{16,0},{32,16},{48,32},{64,48},{80,64},{96,80},{112,96},{128,112},... | collective-permute-start | bytes 1179656 | tf_op jit(solution)/shard_map/ppermute | solution.py:26
  189.3 127.6 %collective-permute-start.7 = (f32[2,4,4,3,1024]{4,3,1,0,2:T(4,128)}, f32[2,4,4,3,1024]{4,3,1,0,2:T(4,128)}, u32[]{:S(2)}, u32[]{:S(2)}) collective-permute-start(f32[2,4,4,3,1024]{4,3,1,0,2:T(4,128)} %get-tuple-element.47), channel_id=1, source_target_pairs={{0,16},{16,32},{32,48},{48,64},{64,80},{80,96},{96,112},{112,128},... | collective-permute-start | bytes 1179656 | tf_op jit(solution)/shard_map/ppermute | solution.py:25
  322.1 1.0 copy-start
  322.2 1.0 copy-start.1
  322.2 1.1 copy-start.2
Sparse Core Ops, SparseCore 0:
  46.9 133.6 all-reduce.4
  188.0 127.8 all-reduce.6
where the time goes:
time: 333 us; the launch traced here: 332 us
  waiting for transfers between devices  277 us (83%)
  other arithmetic  17.9 us (5%)
  between operations  17 us (5%)
  starting transfers between devices  14.5 us (4%)
  local copies, waits for them, and re-layouts  5.4 us (2%)
    psum x2, waiting for transfers between devices, potentials(): totals = lax.psum(partial_value, 'grp') / total_states  253 us
    ppermute x4, waiting for transfers between devices, shifted(): return lax.ppermute(x, axis, [(i, (i + by) % peers) for i in range(peers)])  23.6 us
    ppermute x4, starting transfers between devices, shifted(): return lax.ppermute(x, axis, [(i, (i + by) % peers) for i in range(peers)])  8.4 us
    mul x2, other arithmetic, hamiltonian(): kinetic = -0.5 * (along_depth(extended, planes) + transverse(states, NY))  6.85 us
  transfers between devices with their start and end apart: 10, of which 6 were waited for; matrix products, arithmetic and copies ran while one was open for 2% of the time, Pallas kernels for 0%

commit v1 on v0

v1 whole, which is shorter than its diff:
```python
import functools
import math

import jax
import jax.numpy as jnp
import numpy as np
from jax import lax
from jax.experimental import pallas as pl
from jax.experimental.pallas import tpu as pltpu
from jax.sharding import PartitionSpec as P

MESH = pl.DeviceIdType.MESH
W = (-49.0 / 18.0, 1.5, -0.15, 1.0 / 90.0)
DT = 0.1
NZ = 128
STATES = 64
ONE, THREE, TWO, OWN = 0, 1, 2, 3
ORDER = ((THREE, TWO, ONE, OWN), (OWN, ONE, TWO, THREE))


def stencil_tables(scale):
    lane = lax.broadcasted_iota(jnp.int32, (8, 128), 1)
    sub = lax.broadcasted_iota(jnp.int32, (8, 128), 0)
    y = lane % 32
    w = [scale * v for v in W]
    cy = {}
    for s in (1, -1, 2, -2, 3, -3):
        cy[s] = jnp.where((y + s >= 0) & (y + s < 32), w[abs(s)], 0.0)
    m32 = jnp.where(lane >= 32, w[1], w[3])
    m96 = jnp.where(lane < 96, w[1], w[3])
    up = [jnp.where((lane < 32 * j) & (sub < 7), w[j], 0.0) for j in (1, 2, 3)]
    down = [jnp.where((lane >= 128 - 32 * j) & (sub > 0), w[j], 0.0) for j in (1, 2, 3)]
    return w, cy, m32, m96, up, down


def laplacian(tables, ref, vol, row):
    w, cy, m32, m96, up, down = tables

    def plane(d):
        return ref[vol, pl.ds(pl.multiple_of(row + 8 * d, 8), 8), :]

    f = plane(0)
    t = (3.0 * w[0]) * f
    for j in (1, 2, 3):
        t = t + w[j] * (plane(-j) + plane(j))
    for s in (1, -1, 2, -2, 3, -3):
        t = t + cy[s] * pltpu.roll(f, (-s) % 128, 1)
    r32, r64, r96 = (pltpu.roll(f, 32 * j, 1) for j in (1, 2, 3))
    t = t + m32 * r32 + w[2] * r64 + m96 * r96
    above = up[0] * r32 + up[1] * r64 + up[2] * r96
    below = down[0] * r96 + down[1] * r64 + down[2] * r32
    t = t + pltpu.roll(above, 1, 0) + pltpu.roll(below, 7, 0)
    return f, t


def two_thirds(n):
    y = jnp.exp(jnp.log(jnp.maximum(n, 1e-30)) * (1.0 / 3.0))
    y = y - (y * y * y - n) / (3.0 * y * y)
    return y * y


def kernel(shift_ref, boost_ref, cos_ref, sin_ref, x_ref, o_ref,
           r_buf, e_buf, b_buf, p_buf, d1, rs1, t1, s1, sel1, ag1, f0, acc, d2, rs2, t2, ag2,
           x_sem, slab_send, slab_recv, rs1_send, rs1_recv, s1_send, s1_recv, ag1_send, ag1_recv,
           rs2_send, rs2_recv, ag2_send, ag2_recv, halo_send, halo_recv):
    slabs = lax.axis_size("slab")
    groups = lax.axis_size("grp")
    i = lax.axis_index("slab")
    g = lax.axis_index("grp")
    core = lax.rem(i, 2)
    mate = i + 1 - 2 * core

    def slab(d):
        return (lax.rem(i + d + slabs, slabs), g)

    def peer(k):
        return (i, lax.rem(g + k, groups))

    def own_copy(c):
        return pltpu.make_async_copy(x_ref.at[c], r_buf.at[OWN, c], x_sem.at[c])

    own_copy(0).start()
    own_copy(1).start()

    barrier = pltpu.get_barrier_semaphore()
    for d in (1, -1, 2, -2, 3, -3):
        pl.semaphore_signal(barrier, inc=1, device_id=slab(d), device_id_type=MESH)

    def greet(k, _):
        pl.semaphore_signal(barrier, inc=1, device_id=peer(k), device_id_type=MESH)
        return 0

    lax.fori_loop(1, groups, greet, 0)

    for c in range(2):
        own_copy(c).wait()

        def terms(j, _):
            lanes = pl.ds(pl.multiple_of(j * 128, 128), 128)
            n = kr = ki = None
            for s in range(4):
                ur, ui, vr, vi = (r_buf[OWN, c, s, k, :, lanes] for k in range(4))
                a = vr * vr + vi * vi
                b = ur * vr + ui * vi
                e = ui * vr - ur * vi
                n, kr, ki = (a, b, e) if s == 0 else (n + a, kr + b, ki + e)
            for q, v in enumerate((n, kr, ki)):
                d1[pl.ds(c * 192 + q * 8 + j, 8, stride=24), :] = v
            return 0

        lax.fori_loop(0, 8, terms, 0)

    pl.semaphore_wait(barrier, 6 + groups - 1)

    def rows24(o):
        return pl.ds(pl.multiple_of(o * 24, 8), 24)

    def rs1_copy(k):
        o = lax.rem(g + k, groups)
        return pltpu.make_async_remote_copy(
            src_ref=d1.at[rows24(o)], dst_ref=rs1.at[g], send_sem=rs1_send.at[o], recv_sem=rs1_recv.at[g],
            device_id=peer(k), device_id_type=MESH)

    def start(make):
        def body(k, _):
            make(k).start()
            return 0
        lax.fori_loop(1, groups, body, 0)

    def wait_send(make):
        def body(k, _):
            make(k).wait_send()
            return 0
        lax.fori_loop(1, groups, body, 0)

    def wait_recv(buf, sem):
        def body(k, _):
            o = lax.rem(g + k, groups)
            pltpu.make_async_copy(buf.at[o], buf.at[o], sem.at[o]).wait()
            return 0
        lax.fori_loop(1, groups, body, 0)

    start(rs1_copy)
    rs1[g] = d1[rows24(g), :]

    def far_copy(c, s):
        to = 2 - 4 * c
        return pltpu.make_async_remote_copy(
            src_ref=r_buf.at[OWN, c, s], dst_ref=r_buf.at[TWO, c, s],
            send_sem=slab_send.at[TWO, c, s], recv_sem=slab_recv.at[TWO, c, s],
            device_id=slab(to), device_id_type=MESH)

    def near_copy(s):
        return pltpu.make_async_remote_copy(
            src_ref=r_buf.at[OWN, core, s], dst_ref=r_buf.at[ONE, core, s],
            send_sem=slab_send.at[ONE, core, s], recv_sem=slab_recv.at[ONE, core, s],
            device_id=(mate, g), device_id_type=MESH)

    def third_copy(s):
        return pltpu.make_async_remote_copy(
            src_ref=r_buf.at[OWN, 1 - core, s], dst_ref=r_buf.at[THREE, 1 - core, s],
            send_sem=slab_send.at[THREE, 1 - core, s], recv_sem=slab_recv.at[THREE, 1 - core, s],
            device_id=slab(6 * core - 3), device_id_type=MESH)

    def forward_copy(c, s):
        slot = 1 - (c - core) * (c - core)
        return pltpu.make_async_remote_copy(
            src_ref=r_buf.at[TWO, c, s], dst_ref=r_buf.at[slot, c, s],
            send_sem=slab_send.at[slot, c, s], recv_sem=slab_recv.at[slot, c, s],
            device_id=(mate, g), device_id_type=MESH)

    def start_moves(s, _):
        far_copy(0, s).start()
        far_copy(1, s).start()
        near_copy(s).start()
        third_copy(s).start()
        return 0

    lax.fori_loop(0, 4, start_moves, 0)

    wait_recv(rs1, rs1_recv)

    def add24(k, total):
        return total + rs1[k]

    t1[...] = lax.fori_loop(1, groups, add24, rs1[0])
    cloud = g // 8
    plane_own = lax.rem(g, 8)
    way = 1 - 2 * cloud

    def s1_copy(d):
        return pltpu.make_async_remote_copy(
            src_ref=t1, dst_ref=s1.at[d - 1], send_sem=s1_send.at[d - 1], recv_sem=s1_recv.at[d - 1],
            device_id=slab(way * d), device_id_type=MESH)

    s1_copy(1).start()
    s1_copy(2).start()
    s1_copy(1).wait()
    s1_copy(2).wait()
    r0 = shift_ref[0] - 8
    r1 = shift_ref[1] - 8
    steps = plane_own * way + 7 * cloud + shift_ref[cloud] - 8
    sel1[...] = s1[(steps >> 3) & 1]

    def ag1_copy(k):
        o = lax.rem(g + k, groups)
        return pltpu.make_async_remote_copy(
            src_ref=sel1, dst_ref=ag1.at[g], send_sem=ag1_send.at[o], recv_sem=ag1_recv.at[g],
            device_id=peer(k), device_id_type=MESH)

    start(ag1_copy)
    ag1[g] = sel1[...]
    acc[...] = jnp.zeros_like(acc)
    wait_recv(ag1, ag1_recv)

    def fields_now(p, _):
        z = 8 * i + p
        n = kr = ki = None
        for c in range(2):
            src = 8 * c + ((p - r0 if c == 0 else p + r1) & 7)
            index = (2 * boost_ref[c] * z) & (NZ - 1)
            cos, sin = cos_ref[index], sin_ref[index]
            a, b, e = ag1[src, 0:8, :], ag1[src, 8:16, :], ag1[src, 16:24, :]
            b, e = b * cos - e * sin, b * sin + e * cos
            n, kr, ki = (a, b, e) if c == 0 else (n + a, kr + b, ki + e)
        rows = pl.multiple_of(p * 24, 8)
        f0[pl.ds(rows, 8), :] = DT * (1.2 * two_thirds(n * (1.0 / STATES)) - 1.0)
        f0[pl.ds(rows + 8, 8), :] = kr * (-3.0 * DT / STATES)
        f0[pl.ds(rows + 16, 8), :] = ki * (-3.0 * DT / STATES)
        return 0

    lax.fori_loop(0, 8, fields_now, 0)

    tables = stencil_tables(0.5 * DT)
    e_planes = e_buf.reshape(2, 4, 32, 8, 128)

    def state_step(s, _):
        for c in range(2):
            pltpu.make_async_copy(r_buf.at[TWO, c, s], r_buf.at[TWO, c, s], slab_recv.at[TWO, c, s]).wait()
            forward_copy(c, s).start()
        for c in range(2):
            for slot in (ONE, THREE):
                pltpu.make_async_copy(r_buf.at[slot, c, s], r_buf.at[slot, c, s], slab_recv.at[slot, c, s]).wait()
            order = ORDER[c]
            for k in range(4):
                for j in range(8):
                    lanes = slice(128 * j, 128 * j + 128)
                    e_buf[c, k, pl.ds(6 * 8 + j, 2, stride=8), :] = r_buf[order[0], c, s, k, 6:8, lanes]
                    e_buf[c, k, pl.ds(8 * 8 + j, 8, stride=8), :] = r_buf[order[1], c, s, k, :, lanes]
                    e_buf[c, k, pl.ds(16 * 8 + j, 8, stride=8), :] = r_buf[order[2], c, s, k, :, lanes]
                    e_buf[c, k, pl.ds(24 * 8 + j, 2, stride=8), :] = r_buf[order[3], c, s, k, 0:2, lanes]
            vol = (c * 4 + s) * 4
            base = 13 - r0 if c == 0 else 5 + r1

            def boost(q, _):
                index = (boost_ref[c] * (8 * i + q - 3)) & (NZ - 1)
                cos, sin = cos_ref[index], sin_ref[index]
                ur, ui, vr, vi = (e_planes[c, k, (base + q) & 31] for k in range(4))
                to = pl.ds(pl.multiple_of(q * 8, 8), 8)
                b_buf[vol, to, :] = ur * cos - ui * sin
                b_buf[vol + 1, to, :] = ur * sin + ui * cos
                b_buf[vol + 2, to, :] = vr * cos + vi * sin
                b_buf[vol + 3, to, :] = vi * cos - vr * sin
                return 0

            lax.fori_loop(0, 14, boost, 0)

            def predict(p, _):
                row = pl.multiple_of((p + 3) * 8, 8)
                rows = pl.multiple_of(p * 24, 8)
                pot, dr, di = (f0[pl.ds(rows + 8 * q, 8), :] for q in range(3))
                ur, lur = laplacian(tables, b_buf, vol, row)
                ui, lui = laplacian(tables, b_buf, vol + 1, row)
                vr, lvr = laplacian(tables, b_buf, vol + 2, row)
                vi, lvi = laplacian(tables, b_buf, vol + 3, row)
                pur = ur - lui + (pot * ui + dr * vi + di * vr)
                pui = ui + lur - (pot * ur + dr * vr - di * vi)
                pvr = vr + lvi + (dr * ui - di * ur - pot * vi)
                pvi = vi - lvr - (dr * ur + di * ui - pot * vr)
                at = pl.ds(row, 8)
                p_buf[vol, at, :] = pur
                p_buf[vol + 1, at, :] = pui
                p_buf[vol + 2, at, :] = pvr
                p_buf[vol + 3, at, :] = pvi
                acc[pl.ds(rows, 8), :] += pvr * pvr + pvi * pvi
                acc[pl.ds(rows + 8, 8), :] += pur * pvr + pui * pvi
                acc[pl.ds(rows + 16, 8), :] += pui * pvr - pur * pvi
                return 0

            lax.fori_loop(0, 8, predict, 0)
        return 0

    lax.fori_loop(0, 4, state_step, 0)

    for p in range(8):
        for q in range(3):
            v = acc[p * 24 + q * 8:p * 24 + q * 8 + 8, :]
            d2[p, q] = v[0:4]
            d2[8 + p, q] = v[4:8]

    def rs2_copy(k):
        o = lax.rem(g + k, groups)
        return pltpu.make_async_remote_copy(
            src_ref=d2.at[o], dst_ref=rs2.at[g], send_sem=rs2_send.at[o], recv_sem=rs2_recv.at[g],
            device_id=peer(k), device_id_type=MESH)

    start(rs2_copy)

    def halo_copy(d):
        src = pl.ds(24, 24) if d == 0 else pl.ds(64, 24)
        dst = pl.ds(88, 24) if d == 0 else pl.ds(0, 24)
        return pltpu.make_async_remote_copy(
            src_ref=p_buf.at[:, src], dst_ref=p_buf.at[:, dst], send_sem=halo_send.at[d], recv_sem=halo_recv.at[d],
            device_id=slab(2 * d - 1), device_id_type=MESH)

    halo_copy(0).start()
    halo_copy(1).start()
    rs2[g] = d2[g]
    wait_recv(rs2, rs2_recv)

    def add4(k, total):
        return tuple(total[q] + rs2[k, q] for q in range(3))

    n, kr, ki = lax.fori_loop(1, groups, add4, tuple(rs2[0, q] for q in range(3)))
    t2[0] = DT * (1.2 * two_thirds(n * (1.0 / STATES)) - 1.0)
    t2[1] = kr * (-3.0 * DT / STATES)
    t2[2] = ki * (-3.0 * DT / STATES)

    def ag2_copy(k):
        o = lax.rem(g + k, groups)
        return pltpu.make_async_remote_copy(
            src_ref=t2, dst_ref=ag2.at[g], send_sem=ag2_send.at[o], recv_sem=ag2_recv.at[g],
            device_id=peer(k), device_id_type=MESH)

    start(ag2_copy)
    ag2[g] = t2[...]

    halo_copy(0).wait_recv()
    halo_copy(1).wait_recv()

    def kinetic(m, _):
        vol = (m // 8) * 4
        row = pl.multiple_of((lax.rem(m, 8) + 3) * 8, 8)
        at = pl.ds(row, 8)
        ur, lur = laplacian(tables, p_buf, vol, row)
        ui, lui = laplacian(tables, p_buf, vol + 1, row)
        vr, lvr = laplacian(tables, p_buf, vol + 2, row)
        vi, lvi = laplacian(tables, p_buf, vol + 3, row)
        b_buf[vol, at, :] += ur - lui
        b_buf[vol + 1, at, :] += ui + lur
        b_buf[vol + 2, at, :] += vr + lvi
        b_buf[vol + 3, at, :] += vi - lvr
        return 0

    lax.fori_loop(0, 64, kinetic, 0)

    wait_recv(ag2, ag2_recv)

    def correct(p, _):
        pot, dr, di = (jnp.concatenate([ag2[p, q], ag2[8 + p, q]], axis=0) for q in range(3))
        row = pl.multiple_of((p + 3) * 8, 8)
        at = pl.ds(row, 8)

        def one(m, _):
            vol = m * 4
            ur, ui, vr, vi = (p_buf[vol + k, at, :] for k in range(4))
            gur, gui, gvr, gvi = (b_buf[vol + k, at, :] for k in range(4))
            to = pl.ds(p, 8, stride=8)
            o_ref[vol, to, :] = 0.5 * (gur + (pot * ui + dr * vi + di * vr))
            o_ref[vol + 1, to, :] = 0.5 * (gui - (pot * ur + dr * vr - di * vi))
            o_ref[vol + 2, to, :] = 0.5 * (gvr + (dr * ui - di * ur - pot * vi))
            o_ref[vol + 3, to, :] = 0.5 * (gvi - (dr * ur + di * ui - pot * vr))
            return 0

        lax.fori_loop(0, 8, one, 0)
        return 0

    lax.fori_loop(0, 8, correct, 0)

    wait_send(rs1_copy)
    wait_send(ag1_copy)
    wait_send(rs2_copy)
    wait_send(ag2_copy)
    halo_copy(0).wait_send()
    halo_copy(1).wait_send()

    def moves_sent(s, _):
        near_copy(s).wait_send()
        third_copy(s).wait_send()
        for c in range(2):
            far_copy(c, s).wait_send()
            forward_copy(c, s).wait_send()
        return 0

    lax.fori_loop(0, 4, moves_sent, 0)


def local(cloud_states, cloud_shift, boost_wave):
    f32 = jnp.float32
    angles = 2.0 * math.pi / NZ * np.arange(NZ)
    cos = jnp.asarray(np.cos(angles), f32)
    sin = jnp.asarray(np.sin(angles), f32)
    smem = pl.BlockSpec(memory_space=pltpu.SMEM)
    dma = pltpu.SemaphoreType.DMA
    out = pl.pallas_call(
        kernel,
        out_shape=jax.ShapeDtypeStruct((32, 64, 128), f32),
        in_specs=[smem, smem, smem, smem, pl.BlockSpec(memory_space=pl.ANY)],
        out_specs=pl.BlockSpec(memory_space=pltpu.VMEM),
        scratch_shapes=[
            pltpu.VMEM((4, 2, 4, 4, 8, 1024), f32),
            pltpu.VMEM((2, 4, 256, 128), f32),
            pltpu.VMEM((32, 112, 128), f32),
            pltpu.VMEM((32, 112, 128), f32),
            pltpu.VMEM((384, 128), f32),
            pltpu.VMEM((16, 24, 128), f32),
            pltpu.VMEM((24, 128), f32),
            pltpu.VMEM((2, 24, 128), f32),
            pltpu.VMEM((24, 128), f32),
            pltpu.VMEM((16, 24, 128), f32),
            pltpu.VMEM((192, 128), f32),
            pltpu.VMEM((192, 128), f32),
            pltpu.VMEM((16, 3, 4, 128), f32),
            pltpu.VMEM((16, 3, 4, 128), f32),
            pltpu.VMEM((3, 4, 128), f32),
            pltpu.VMEM((16, 3, 4, 128), f32),
            dma((2,)), dma((3, 2, 4)), dma((3, 2, 4)),
            dma((16,)), dma((16,)), dma((2,)), dma((2,)), dma((16,)), dma((16,)),
            dma((16,)), dma((16,)), dma((16,)), dma((16,)), dma((2,)), dma((2,)),
        ],
        compiler_params=pltpu.CompilerParams(
            collective_id=0, has_side_effects=True, vmem_limit_bytes=40 * 2**20),
    )(cloud_shift, boost_wave, cos, sin, cloud_states)
    out = out.reshape(2, 4, 4, 8, 8, 128).transpose(0, 1, 2, 4, 3, 5)
    return out.reshape(2, 4, 4, 8, 1024)


def solution(mesh):
    in_specs = (P(None, "grp", None, "slab", None), P(), P())
    out_specs = P(None, "grp", None, "slab", None)
    return jax.shard_map(local, mesh=mesh, in_specs=in_specs, out_specs=out_specs, check_vma=False)
```

time: 333 us -> 89.1 us (0.27)
  waiting for transfers between devices: 277 us -> 0 us
  Pallas kernels: 0 us -> 83.1 us
  other arithmetic: 17.9 us -> 0 us
  between operations: 17 us -> 0.01 us
  starting transfers between devices: 14.5 us -> 0 us
    psum x2 -> x0, waiting for transfers between devices: 253 us -> none  [potentials(): totals = lax.psum(partial_value, 'grp') / total_states]
    pallas_call x0 -> x1, Pallas kernels: none -> 83.1 us  [local(): pl.pallas_call(kernel, out_shape=jax.ShapeDtypeStruct((32, 64, 128), f32)...]
    ppermute x8 -> x0, waiting for transfers between devices: 23.6 us -> none  [the longest x4 23.6 us: shifted(): return lax.ppermute(x, axis, [(i, (i + by) % peers) for i in range(peers)])]
    ppermute x8 -> x0, starting transfers between devices: 14.4 us -> none  [the longest x4 8.4 us: shifted(): return lax.ppermute(x, axis, [(i, (i + by) % peers) for i in range(peers)])]
    mul x3 -> x0, other arithmetic: 6.9 us -> none  [the longest x2 6.85 us: hamiltonian(): kinetic = -0.5 * (along_depth(extended, planes) + transverse(states, NY))]
    unnamed x18 -> x11, local copies, waits for them, and re-layouts: 0.92 us -> 4.82 us
  transfers between devices with their start and end apart: 10 -> 0, of which waited for: 6 -> 0; matrix products, arithmetic and copies ran while one was open for 2% -> 0% of each run, Pallas kernels for 0% -> 0%
where the time goes in v1:
time: 89.1 us; the launch traced here: 87.9 us
  Pallas kernels  83.1 us (93%)
  local copies, waits for them, and re-layouts  4.82 us (5%)
    pallas_call x1, Pallas kernels, local(): pl.pallas_call(kernel, out_shape=jax.ShapeDtypeStruct((32, 64, 128), f32)...  83.1 us
    unnamed x11, local copies, waits for them, and re-layouts  4.82 us

profile of v1, /device:TPU:2, one launch (start us, length us, event | category | flops | bytes accessed | tf_op | source)
XLA Modules:
  0.0 87.9 jit_solution(18117532359144977663)
XLA Ops:
  0.0 0.0 copy-start.3
  0.0 0.7 copy-done.3
  0.7 0.0 copy-start
  0.7 1.2 %copy-done = f32[2,4,4,8,1024]{4,3,2,1,0:T(8,128)S(1)} copy-done((f32[2,4,4,8,1024]{4,3,2,1,0:T(8,128)S(1)}, f32[2,4,4,8,1024]{4,3,2,1,0:T(8,128)}, u32[]{:S(2)}) %copy-start) | copy-done | bytes 1048600
  1.9 0.0 copy-start.1
  1.9 0.7 copy-done.1
  2.5 0.0 copy-start.2
  2.5 0.7 copy-done.2
  3.2 0.0 copy-start.4
  3.2 0.7 copy-done.4
  3.8 83.1 %shard_map.55 = f32[32,64,128]{2,1,0:T(8,128)S(1)} custom-call(s32[2]{0:T(128)S(1)} %copy-done.1, s32[2]{0:T(128)S(1)} %copy-done.2, f32[128]{0:T(128)S(1)} %copy-done.4, f32[128]{0:T(128)S(1)} %copy-done.3, f32[2,4,4,8,1024]{4,3,2,1,0:T(8,128)S(1)} %copy-done), custom_call_target="tpu_custom_call" | custom-call | tf_op jit(solution)/shard_map/pallas_call | solution.py:405
  86.9 1.0 %copy.7 = f32[2,4,4,8,1024]{4,3,2,1,0:T(8,128)} copy(f32[2,4,4,8,1024]{4,3,2,1,0:T(8,128)S(1)} %bitcast.5) | data formatting | bytes 2097152
Async XLA Ops:
  0.0 0.7 copy-start.3
  0.7 1.2 %copy-start = (f32[2,4,4,8,1024]{4,3,2,1,0:T(8,128)S(1)}, f32[2,4,4,8,1024]{4,3,2,1,0:T(8,128)}, u32[]{:S(2)}) copy-start(f32[2,4,4,8,1024]{4,3,2,1,0:T(8,128)} %x_ref.1) | copy-start | bytes 3145732
  1.9 0.7 copy-start.1
  2.5 0.7 copy-start.2
  3.2 0.7 copy-start.4

commit v2 on v1

v2 whole, which is shorter than its diff:
```python
import math

import jax
import jax.numpy as jnp
from jax import lax
from jax.experimental import pallas as pl
from jax.experimental.pallas import tpu as pltpu
from jax.sharding import PartitionSpec as P

MESH = pl.DeviceIdType.MESH
W = (-49.0 / 18.0, 1.5, -0.15, 1.0 / 90.0)
DT = 0.1
VMEM_LIMIT = 60 * 2**20
NZ = 128
STATES = 64
M = 4
ONE, THREE, TWO = 0, 1, 2


def stencil_tables(scale):
    lane = lax.broadcasted_iota(jnp.int32, (8, 128), 1)
    sub = lax.broadcasted_iota(jnp.int32, (8, 128), 0)
    y = lane % 32
    w = [scale * v for v in W]
    cy = {}
    for s in (1, -1, 2, -2, 3, -3):
        cy[s] = jnp.where((y + s >= 0) & (y + s < 32), w[abs(s)], 0.0)
    m32 = jnp.where(lane >= 32, w[1], w[3])
    m96 = jnp.where(lane < 96, w[1], w[3])
    up = [jnp.where((lane < 32 * j) & (sub < 7), w[j], 0.0) for j in (1, 2, 3)]
    down = [jnp.where((lane >= 128 - 32 * j) & (sub > 0), w[j], 0.0) for j in (1, 2, 3)]
    return w, cy, m32, m96, up, down


def laplacian(tables, ref, vol, row):
    w, cy, m32, m96, up, down = tables

    def plane(d):
        return ref[vol, pl.ds(pl.multiple_of(row + 8 * d, 8), 8 * M), :].reshape(M, 8, 128)

    f = plane(0)
    t = (3.0 * w[0]) * f
    for j in (1, 2, 3):
        t = t + w[j] * (plane(-j) + plane(j))
    for s in (1, -1, 2, -2, 3, -3):
        t = t + cy[s] * pltpu.roll(f, (-s) % 128, 2)
    r32, r64, r96 = (pltpu.roll(f, 32 * j, 2) for j in (1, 2, 3))
    t = t + m32 * r32 + w[2] * r64 + m96 * r96
    above = up[0] * r32 + up[1] * r64 + up[2] * r96
    below = down[0] * r96 + down[1] * r64 + down[2] * r32
    return f, t + pltpu.roll(above, 1, 1) + pltpu.roll(below, 7, 1)


def two_thirds(n):
    y = jnp.exp(jnp.log(jnp.maximum(n, 1e-30)) * (1.0 / 3.0))
    y = y - (y * y * y - n) / (3.0 * y * y)
    return y * y


def kernel(shift_ref, boost_ref, x_ref, o_ref,
           x_buf, land, e_buf, b_buf, p_buf, trig, d1, rs1, t1, s1, sel1, ag1, f0, acc, d2, rs2, t2, ag2,
           x_sem, slab_send, slab_recv, rs1_send, rs1_recv, s1_send, s1_recv, ag1_send, ag1_recv,
           rs2_send, rs2_recv, ag2_send, ag2_recv, halo_send, halo_recv):
    slabs = lax.axis_size("slab")
    groups = lax.axis_size("grp")
    i = lax.axis_index("slab")
    g = lax.axis_index("grp")
    core = lax.rem(i, 2)
    mate = i + 1 - 2 * core

    def slab(d):
        return (lax.rem(i + d + slabs, slabs), g)

    def peer(k):
        return (i, lax.rem(g + k, groups))

    def own_copy(c):
        return pltpu.make_async_copy(x_ref.at[c], x_buf.at[c], x_sem.at[c])

    own_copy(0).start()
    own_copy(1).start()

    barrier = pltpu.get_barrier_semaphore()
    for d in (1, -1, 2, -2, 3, -3):
        pl.semaphore_signal(barrier, inc=1, device_id=slab(d), device_id_type=MESH)

    def greet(k, _):
        pl.semaphore_signal(barrier, inc=1, device_id=peer(k), device_id_type=MESH)
        return 0

    lax.fori_loop(1, groups, greet, 0)

    for c in range(2):
        own_copy(c).wait()

        def relay(m, _):
            s = m // 4
            k = lax.rem(m, 4)
            for j in range(8):
                land[c, s, k, pl.ds(192 - 192 * c + j, 8, stride=8), :] = x_buf[c, s, k, :, 128 * j:128 * j + 128]
            return 0

        lax.fori_loop(0, 16, relay, 0)

        def terms(p, _):
            at = pl.ds(pl.multiple_of(192 - 192 * c + 8 * p, 8), 8)
            n = kr = ki = None
            for s in range(4):
                ur, ui, vr, vi = (land[c, s, k, at, :] for k in range(4))
                a = vr * vr + vi * vi
                b = ur * vr + ui * vi
                e = ui * vr - ur * vi
                n, kr, ki = (a, b, e) if s == 0 else (n + a, kr + b, ki + e)
            for q, v in enumerate((n, kr, ki)):
                d1[c * 8 + p, q] = v
            return 0

        lax.fori_loop(0, 8, terms, 0)

    def phases(m, _):
        c = m // 14
        q = lax.rem(m, 14)
        index = (boost_ref[c] * (8 * i + q - 3)) & (NZ - 1)
        angle = jnp.full((8, 128), index, jnp.int32).astype(jnp.float32) * (2.0 * math.pi / NZ)
        trig[c, q, 0] = jnp.cos(angle)
        trig[c, q, 1] = jnp.sin(angle)
        return 0

    lax.fori_loop(0, 28, phases, 0)
    acc[...] = jnp.zeros_like(acc)

    pl.semaphore_wait(barrier, 6 + groups - 1)

    def start(make):
        def body(k, _):
            make(k).start()
            return 0
        lax.fori_loop(1, groups, body, 0)

    def wait_send(make):
        def body(k, _):
            make(k).wait_send()
            return 0
        lax.fori_loop(1, groups, body, 0)

    def wait_recv(buf, sem):
        def body(k, _):
            o = lax.rem(g + k, groups)
            pltpu.make_async_copy(buf.at[o], buf.at[o], sem.at[o]).wait()
            return 0
        lax.fori_loop(1, groups, body, 0)

    def scatter(src, dst, send, recv):
        def make(k):
            o = lax.rem(g + k, groups)
            return pltpu.make_async_remote_copy(
                src_ref=src.at[o], dst_ref=dst.at[g], send_sem=send.at[o], recv_sem=recv.at[g],
                device_id=peer(k), device_id_type=MESH)
        return make

    def gather(src, dst, send, recv):
        def make(k):
            o = lax.rem(g + k, groups)
            return pltpu.make_async_remote_copy(
                src_ref=src, dst_ref=dst.at[g], send_sem=send.at[o], recv_sem=recv.at[g],
                device_id=peer(k), device_id_type=MESH)
        return make

    rs1_copy = scatter(d1, rs1, rs1_send, rs1_recv)
    ag1_copy = gather(sel1, ag1, ag1_send, ag1_recv)
    rs2_copy = scatter(d2, rs2, rs2_send, rs2_recv)
    ag2_copy = gather(t2, ag2, ag2_send, ag2_recv)

    def window(c, s, first, planes):
        return land.at[c, s, :, pl.ds(pl.multiple_of(first * 8, 8), planes * 8)]

    def move(slot, c, s, src, dst, planes, device):
        return pltpu.make_async_remote_copy(
            src_ref=window(c, s, src, planes), dst_ref=window(c, s, dst, planes),
            send_sem=slab_send.at[slot, c, s], recv_sem=slab_recv.at[slot, c, s],
            device_id=device, device_id_type=MESH)

    def far_copy(c, s):
        return move(TWO, c, s, 24 - 24 * c, 8 + 8 * c, 8, slab(2 - 4 * c))

    def near_copy(s):
        return move(ONE, core, s, 24 - 24 * core, 16 - 8 * core, 8, (mate, g))

    def third_copy(s):
        return move(THREE, 1 - core, s, 30 * core, 24 - 18 * core, 2, slab(6 * core - 3))

    def forward_one(s):
        return move(ONE, 1 - core, s, 16 - 8 * core, 8 + 8 * core, 8, (mate, g))

    def forward_three(s):
        return move(THREE, core, s, 14 + 2 * core, 6 + 18 * core, 2, (mate, g))

    def arrived(slot, c, s, planes):
        here = window(c, s, 0, planes)
        pltpu.make_async_copy(here, here, slab_recv.at[slot, c, s]).wait()

    def start_moves(s, _):
        far_copy(0, s).start()
        far_copy(1, s).start()
        near_copy(s).start()
        third_copy(s).start()
        return 0

    def forward(s):
        arrived(TWO, 0, s, 8)
        arrived(TWO, 1, s, 8)
        forward_one(s).start()
        forward_three(s).start()

    start(rs1_copy)
    lax.fori_loop(0, 4, start_moves, 0)
    rs1[g] = d1[g]

    wait_recv(rs1, rs1_recv)

    def add1(k, total):
        return total + rs1[k]

    t1[...] = lax.fori_loop(1, groups, add1, rs1[0])
    cloud = g // 8
    plane_own = lax.rem(g, 8)
    way = 1 - 2 * cloud

    def s1_copy(d):
        return pltpu.make_async_remote_copy(
            src_ref=t1, dst_ref=s1.at[d - 1], send_sem=s1_send.at[d - 1], recv_sem=s1_recv.at[d - 1],
            device_id=slab(way * d), device_id_type=MESH)

    s1_copy(1).start()
    s1_copy(2).start()
    forward(0)
    s1_copy(1).wait_recv()
    s1_copy(2).wait_recv()
    r0 = shift_ref[0] - 8
    r1 = shift_ref[1] - 8
    steps = plane_own * way + 7 * cloud + shift_ref[cloud] - 8
    sel1[...] = s1[(steps >> 3) & 1]
    start(ag1_copy)
    ag1[g] = sel1[...]
    forward(1)
    wait_recv(ag1, ag1_recv)

    def fields_now(p, _):
        n = kr = ki = None
        for c in range(2):
            src = 8 * c + ((p - r0 if c == 0 else p + r1) & 7)
            cos, sin = trig[c, p + 3, 0], trig[c, p + 3, 1]
            cos, sin = cos * cos - sin * sin, 2.0 * cos * sin
            a, b, e = ag1[src, 0], ag1[src, 1], ag1[src, 2]
            b, e = b * cos - e * sin, b * sin + e * cos
            n, kr, ki = (a, b, e) if c == 0 else (n + a, kr + b, ki + e)
        f0[0, p] = DT * (1.2 * two_thirds(n * (1.0 / STATES)) - 1.0)
        f0[1, p] = kr * (-3.0 * DT / STATES)
        f0[2, p] = ki * (-3.0 * DT / STATES)
        return 0

    lax.fori_loop(0, 8, fields_now, 0)

    tables = stencil_tables(0.5 * DT)

    def halo_copy(d, s):
        src = pl.ds(24, 24) if d == 0 else pl.ds(64, 24)
        dst = pl.ds(88, 24) if d == 0 else pl.ds(0, 24)
        vols = pl.ds(s * 8, 8)
        return pltpu.make_async_remote_copy(
            src_ref=p_buf.at[vols, src], dst_ref=p_buf.at[vols, dst],
            send_sem=halo_send.at[d, s], recv_sem=halo_recv.at[d, s],
            device_id=slab(2 * d - 1), device_id_type=MESH)

    def send_halos(s):
        halo_copy(0, s).start()
        halo_copy(1, s).start()

    def state_step(s, _):
        for c in range(2):
            arrived(ONE, c, s, 8)
            arrived(THREE, c, s, 2)
            for k in range(4):
                e_buf[k] = land[c, s, k, 48:208, :].reshape(20, 8, 128)
            vol = (s * 2 + c) * 4
            base = 7 - r0 if c == 0 else r1 - 1

            def boost(q, _):
                cos, sin = trig[c, q, 0], trig[c, q, 1]
                plane = jnp.maximum(jnp.minimum(base + q, 19), 0)
                ur, ui, vr, vi = (e_buf[k, plane] for k in range(4))
                to = pl.ds(pl.multiple_of(q * 8, 8), 8)
                b_buf[vol, to, :] = ur * cos - ui * sin
                b_buf[vol + 1, to, :] = ur * sin + ui * cos
                b_buf[vol + 2, to, :] = vr * cos + vi * sin
                b_buf[vol + 3, to, :] = vi * cos - vr * sin
                return 0

            lax.fori_loop(0, 14, boost, 0)

            def predict(m, _):
                p = m * M
                row = pl.multiple_of((p + 3) * 8, 8)
                pot, dr, di = (f0[q, pl.ds(p, M)] for q in range(3))
                ur, lur = laplacian(tables, b_buf, vol, row)
                ui, lui = laplacian(tables, b_buf, vol + 1, row)
                vr, lvr = laplacian(tables, b_buf, vol + 2, row)
                vi, lvi = laplacian(tables, b_buf, vol + 3, row)
                pur = ur - lui + (pot * ui + dr * vi + di * vr)
                pui = ui + lur - (pot * ur + dr * vr - di * vi)
                pvr = vr + lvi + (dr * ui - di * ur - pot * vi)
                pvi = vi - lvr - (dr * ur + di * ui - pot * vr)
                at = pl.ds(row, 8 * M)
                for k, v in enumerate((pur, pui, pvr, pvi)):
                    p_buf[vol + k, at, :] = v.reshape(8 * M, 128)
                acc[0, pl.ds(p, M)] += pvr * pvr + pvi * pvi
                acc[1, pl.ds(p, M)] += pur * pvr + pui * pvi
                acc[2, pl.ds(p, M)] += pui * pvr - pur * pvi
                return 0

            lax.fori_loop(0, 8 // M, predict, 0)

        @pl.when(s < 2)
        def _():
            forward(s + 2)

        @pl.when(s == 1)
        def _():
            send_halos(0)
            send_halos(1)

        @pl.when(s == 2)
        def _():
            send_halos(2)

        return 0

    lax.fori_loop(0, 4, state_step, 0)

    for p in range(8):
        for q in range(3):
            v = acc[q, p]
            d2[p, q] = v[0:4]
            d2[8 + p, q] = v[4:8]

    start(rs2_copy)
    send_halos(3)
    rs2[g] = d2[g]
    wait_recv(rs2, rs2_recv)

    def add2(k, total):
        return total + rs2[k]

    n, kr, ki = lax.fori_loop(1, groups, add2, rs2[0])
    t2[0] = DT * (1.2 * two_thirds(n * (1.0 / STATES)) - 1.0)
    t2[1] = kr * (-3.0 * DT / STATES)
    t2[2] = ki * (-3.0 * DT / STATES)
    start(ag2_copy)
    ag2[g] = t2[...]

    def kinetic_state(s, _):
        halo_copy(0, s).wait_recv()
        halo_copy(1, s).wait_recv()

        def kinetic(m, _):
            vol = (s * 2 + m // (8 // M)) * 4
            row = pl.multiple_of((lax.rem(m, 8 // M) * M + 3) * 8, 8)
            at = pl.ds(row, 8 * M)
            ur, lur = laplacian(tables, p_buf, vol, row)
            ui, lui = laplacian(tables, p_buf, vol + 1, row)
            vr, lvr = laplacian(tables, p_buf, vol + 2, row)
            vi, lvi = laplacian(tables, p_buf, vol + 3, row)
            for k, v in enumerate((ur - lui, ui + lur, vr + lvi, vi - lvr)):
                b_buf[vol + k, at, :] += v.reshape(8 * M, 128)
            return 0

        lax.fori_loop(0, 16 // M, kinetic, 0)
        return 0

    lax.fori_loop(0, 4, kinetic_state, 0)
    wait_recv(ag2, ag2_recv)

    def correct(p, _):
        pot, dr, di = (jnp.concatenate([ag2[p, q], ag2[8 + p, q]], axis=0) for q in range(3))
        at = pl.ds(pl.multiple_of((p + 3) * 8, 8), 8)
        to = pl.ds(p, 8, stride=8)
        for s in range(4):
            for c in range(2):
                vol = (s * 2 + c) * 4
                out = (c * 4 + s) * 4
                ur, ui, vr, vi = (p_buf[vol + k, at, :] for k in range(4))
                gur, gui, gvr, gvi = (b_buf[vol + k, at, :] for k in range(4))
                o_ref[out, to, :] = 0.5 * (gur + (pot * ui + dr * vi + di * vr))
                o_ref[out + 1, to, :] = 0.5 * (gui - (pot * ur + dr * vr - di * vi))
                o_ref[out + 2, to, :] = 0.5 * (gvr + (dr * ui - di * ur - pot * vi))
                o_ref[out + 3, to, :] = 0.5 * (gvi - (dr * ur + di * ui - pot * vr))
        return 0

    lax.fori_loop(0, 8, correct, 0)

    for make in (rs1_copy, ag1_copy, rs2_copy, ag2_copy):
        wait_send(make)
    s1_copy(1).wait_send()
    s1_copy(2).wait_send()

    def moves_sent(s, _):
        for c in range(2):
            far_copy(c, s).wait_send()
            halo_copy(c, s).wait_send()
        near_copy(s).wait_send()
        third_copy(s).wait_send()
        forward_one(s).wait_send()
        forward_three(s).wait_send()
        return 0

    lax.fori_loop(0, 4, moves_sent, 0)


def local(cloud_states, cloud_shift, boost_wave):
    f32 = jnp.float32
    smem = pl.BlockSpec(memory_space=pltpu.SMEM)
    dma = pltpu.SemaphoreType.DMA
    out = pl.pallas_call(
        kernel,
        out_shape=jax.ShapeDtypeStruct((32, 64, 128), f32),
        in_specs=[smem, smem, pl.BlockSpec(memory_space=pl.ANY)],
        out_specs=pl.BlockSpec(memory_space=pltpu.VMEM),
        scratch_shapes=[
            pltpu.VMEM((2, 4, 4, 8, 1024), f32),
            pltpu.VMEM((2, 4, 4, 256, 128), f32),
            pltpu.VMEM((4, 20, 8, 128), f32),
            pltpu.VMEM((32, 112, 128), f32),
            pltpu.VMEM((32, 112, 128), f32),
            pltpu.VMEM((2, 14, 2, 8, 128), f32),
            pltpu.VMEM((16, 3, 8, 128), f32),
            pltpu.VMEM((16, 3, 8, 128), f32),
            pltpu.VMEM((3, 8, 128), f32),
            pltpu.VMEM((2, 3, 8, 128), f32),
            pltpu.VMEM((3, 8, 128), f32),
            pltpu.VMEM((16, 3, 8, 128), f32),
            pltpu.VMEM((3, 8, 8, 128), f32),
            pltpu.VMEM((3, 8, 8, 128), f32),
            pltpu.VMEM((16, 3, 4, 128), f32),
            pltpu.VMEM((16, 3, 4, 128), f32),
            pltpu.VMEM((3, 4, 128), f32),
            pltpu.VMEM((16, 3, 4, 128), f32),
            dma((2,)), dma((3, 2, 4)), dma((3, 2, 4)),
            dma((16,)), dma((16,)), dma((2,)), dma((2,)), dma((16,)), dma((16,)),
            dma((16,)), dma((16,)), dma((16,)), dma((16,)), dma((2, 4)), dma((2, 4)),
        ],
        compiler_params=pltpu.CompilerParams(
            collective_id=0, has_side_effects=True, vmem_limit_bytes=VMEM_LIMIT),
    )(cloud_shift, boost_wave, cloud_states)
    out = out.reshape(2, 4, 4, 8, 8, 128).transpose(0, 1, 2, 4, 3, 5)
    return out.reshape(2, 4, 4, 8, 1024)


def solution(mesh):
    in_specs = (P(None, "grp", None, "slab", None), P(), P())
    out_specs = P(None, "grp", None, "slab", None)
    return jax.shard_map(local, mesh=mesh, in_specs=in_specs, out_specs=out_specs, check_vma=False)
```

time: 89.1 us -> 69.7 us (0.78); the launches traced: 87.9 us -> 69.6 us
  Pallas kernels: 83.1 us -> 67.2 us
  local copies, waits for them, and re-layouts: 4.82 us -> 2.31 us
    pallas_call x1, Pallas kernels: 83.1 us -> 67.2 us  [local(): pl.pallas_call(kernel, out_shape=jax.ShapeDtypeStruct((32, 64, 128), f32)...]
    unnamed x11 -> x1, local copies, waits for them, and re-layouts: 4.82 us -> 2.31 us
where the time goes in v2:
time: 69.7 us; the launch traced here: 69.6 us
  Pallas kernels  67.2 us (96%)
  local copies, waits for them, and re-layouts  2.31 us (3%)
    pallas_call x1, Pallas kernels, local(): pl.pallas_call(kernel, out_shape=jax.ShapeDtypeStruct((32, 64, 128), f32)...  67.2 us
    unnamed x1, local copies, waits for them, and re-layouts  2.31 us

profile of v2, /device:TPU:2, one launch (start us, length us, event | category | flops | bytes accessed | tf_op | source)
XLA Modules:
  0.0 69.6 jit_solution(9788440926168632406)
XLA Ops:
  0.0 67.2 %shard_map.37 = f32[32,64,128]{2,1,0:T(8,128)} custom-call(s32[2]{0:T(128)} %shift_ref.1, s32[2]{0:T(128)} %boost_ref.1, f32[2,4,4,8,1024]{4,3,2,1,0:T(8,128)} %x_ref.1), custom_call_target="tpu_custom_call" | custom-call | tf_op jit(solution)/shard_map/pallas_call | solution.py:423
  67.3 2.3 %copy.5 = f32[2,4,4,8,1024]{4,3,2,1,0:T(8,128)} copy(f32[2,4,4,8,1024]{4,3,2,1,0:T(8,128)} %bitcast.5) | data formatting | bytes 2097152

commit v3 on v2

--- a/solution.py
+++ b/solution.py
@@ -10,7 +10,7 @@
 MESH = pl.DeviceIdType.MESH
 W = (-49.0 / 18.0, 1.5, -0.15, 1.0 / 90.0)
 DT = 0.1
-VMEM_LIMIT = 60 * 2**20
+VMEM_LIMIT = 44 * 2**20
 NZ = 128
 STATES = 64
 M = 4
@@ -83,6 +83,8 @@
     barrier = pltpu.get_barrier_semaphore()
     for d in (1, -1, 2, -2, 3, -3):
         pl.semaphore_signal(barrier, inc=1, device_id=slab(d), device_id_type=MESH)
+    for d in (1, -1, 2, -2):
+        pl.semaphore_signal(barrier, inc=1, device_id=(slab(d)[0], lax.rem(g + 8, groups)), device_id_type=MESH)
 
     def greet(k, _):
         pl.semaphore_signal(barrier, inc=1, device_id=peer(k), device_id_type=MESH)
@@ -112,7 +114,7 @@
                 e = ui * vr - ur * vi
                 n, kr, ki = (a, b, e) if s == 0 else (n + a, kr + b, ki + e)
             for q, v in enumerate((n, kr, ki)):
-                d1[c * 8 + p, q] = v
+                d1[p, c, q] = v
             return 0
 
         lax.fori_loop(0, 8, terms, 0)
@@ -129,47 +131,49 @@
     lax.fori_loop(0, 28, phases, 0)
     acc[...] = jnp.zeros_like(acc)
 
-    pl.semaphore_wait(barrier, 6 + groups - 1)
-
-    def start(make):
+    pl.semaphore_wait(barrier, 10 + groups - 1)
+
+    column = g // 8
+    z_own = lax.rem(g, 8)
+
+    def in_group(k):
+        return lax.rem(g + k, groups)
+
+    def in_column(k):
+        return column * 8 + lax.rem(z_own + k, 8)
+
+    def start(make, count):
         def body(k, _):
             make(k).start()
             return 0
-        lax.fori_loop(1, groups, body, 0)
-
-    def wait_send(make):
+        lax.fori_loop(1, count, body, 0)
+
+    def wait_send(make, count):
         def body(k, _):
             make(k).wait_send()
             return 0
-        lax.fori_loop(1, groups, body, 0)
-
-    def wait_recv(buf, sem):
+        lax.fori_loop(1, count, body, 0)
+
+    def wait_recv(buf, sem, count, mine):
         def body(k, _):
-            o = lax.rem(g + k, groups)
+            o = lax.rem(mine + k, count)
             pltpu.make_async_copy(buf.at[o], buf.at[o], sem.at[o]).wait()
             return 0
-        lax.fori_loop(1, groups, body, 0)
-
-    def scatter(src, dst, send, recv):
+        lax.fori_loop(1, count, body, 0)
+
+    def exchange(src, dst, send, recv, one, count, mine):
         def make(k):
-            o = lax.rem(g + k, groups)
+            o = lax.rem(mine + k, count)
+            to = in_group(k) if count == groups else in_column(k)
             return pltpu.make_async_remote_copy(
-                src_ref=src.at[o], dst_ref=dst.at[g], send_sem=send.at[o], recv_sem=recv.at[g],
-                device_id=peer(k), device_id_type=MESH)
+                src_ref=src if one else src.at[o], dst_ref=dst.at[mine], send_sem=send.at[o], recv_sem=recv.at[mine],
+                device_id=(i, to), device_id_type=MESH)
         return make
 
-    def gather(src, dst, send, recv):
-        def make(k):
-            o = lax.rem(g + k, groups)
-            return pltpu.make_async_remote_copy(
-                src_ref=src, dst_ref=dst.at[g], send_sem=send.at[o], recv_sem=recv.at[g],
-                device_id=peer(k), device_id_type=MESH)
-        return make
-
-    rs1_copy = scatter(d1, rs1, rs1_send, rs1_recv)
-    ag1_copy = gather(sel1, ag1, ag1_send, ag1_recv)
-    rs2_copy = scatter(d2, rs2, rs2_send, rs2_recv)
-    ag2_copy = gather(t2, ag2, ag2_send, ag2_recv)
+    rs1_copy = exchange(d1, rs1, rs1_send, rs1_recv, False, 8, z_own)
+    ag1_copy = exchange(sel1, ag1, ag1_send, ag1_recv, True, 8, z_own)
+    rs2_copy = exchange(d2, rs2, rs2_send, rs2_recv, False, groups, g)
+    ag2_copy = exchange(t2, ag2, ag2_send, ag2_recv, True, groups, g)
 
     def window(c, s, first, planes):
         return land.at[c, s, :, pl.ds(pl.multiple_of(first * 8, 8), planes * 8)]
@@ -212,46 +216,46 @@
         forward_one(s).start()
         forward_three(s).start()
 
-    start(rs1_copy)
+    start(rs1_copy, 8)
     lax.fori_loop(0, 4, start_moves, 0)
-    rs1[g] = d1[g]
-
-    wait_recv(rs1, rs1_recv)
+    rs1[z_own] = d1[z_own]
+
+    wait_recv(rs1, rs1_recv, 8, z_own)
 
     def add1(k, total):
         return total + rs1[k]
 
-    t1[...] = lax.fori_loop(1, groups, add1, rs1[0])
-    cloud = g // 8
-    plane_own = lax.rem(g, 8)
-    way = 1 - 2 * cloud
-
-    def s1_copy(d):
+    t1[...] = lax.fori_loop(1, 8, add1, rs1[0])
+
+    def s1_copy(c, d, x):
         return pltpu.make_async_remote_copy(
-            src_ref=t1, dst_ref=s1.at[d - 1], send_sem=s1_send.at[d - 1], recv_sem=s1_recv.at[d - 1],
-            device_id=slab(way * d), device_id_type=MESH)
-
-    s1_copy(1).start()
-    s1_copy(2).start()
+            src_ref=t1.at[c], dst_ref=s1.at[c, d, column], send_sem=s1_send.at[c, d, x], recv_sem=s1_recv.at[c, d, column],
+            device_id=(slab((1 - 2 * c) * (d + 1))[0], x * 8 + z_own), device_id_type=MESH)
+
+    cases = [(c, d, x) for c in range(2) for d in range(2) for x in range(2)]
+    for case in cases:
+        s1_copy(*case).start()
     forward(0)
-    s1_copy(1).wait_recv()
-    s1_copy(2).wait_recv()
+    for c, d, x in cases:
+        pltpu.make_async_copy(s1.at[c, d, x], s1.at[c, d, x], s1_recv.at[c, d, x]).wait()
     r0 = shift_ref[0] - 8
     r1 = shift_ref[1] - 8
-    steps = plane_own * way + 7 * cloud + shift_ref[cloud] - 8
-    sel1[...] = s1[(steps >> 3) & 1]
-    start(ag1_copy)
-    ag1[g] = sel1[...]
+    from_0 = ((z_own + r0) >> 3) & 1
+    from_1 = ((7 - z_own + r1) >> 3) & 1
+    sel1[0] = s1[0, from_0, 0] + s1[0, from_0, 1]
+    sel1[1] = s1[1, from_1, 0] + s1[1, from_1, 1]
+    start(ag1_copy, 8)
+    ag1[z_own] = sel1[...]
     forward(1)
-    wait_recv(ag1, ag1_recv)
+    wait_recv(ag1, ag1_recv, 8, z_own)
 
     def fields_now(p, _):
         n = kr = ki = None
         for c in range(2):
-            src = 8 * c + ((p - r0 if c == 0 else p + r1) & 7)
+            src = (p - r0 if c == 0 else p + r1) & 7
             cos, sin = trig[c, p + 3, 0], trig[c, p + 3, 1]
             cos, sin = cos * cos - sin * sin, 2.0 * cos * sin
-            a, b, e = ag1[src, 0], ag1[src, 1], ag1[src, 2]
+            a, b, e = ag1[src, c, 0], ag1[src, c, 1], ag1[src, c, 2]
             b, e = b * cos - e * sin, b * sin + e * cos
             n, kr, ki = (a, b, e) if c == 0 else (n + a, kr + b, ki + e)
         f0[0, p] = DT * (1.2 * two_thirds(n * (1.0 / STATES)) - 1.0)
@@ -343,10 +347,10 @@
             d2[p, q] = v[0:4]
             d2[8 + p, q] = v[4:8]
 
-    start(rs2_copy)
+    start(rs2_copy, groups)
     send_halos(3)
     rs2[g] = d2[g]
-    wait_recv(rs2, rs2_recv)
+    wait_recv(rs2, rs2_recv, groups, g)
 
     def add2(k, total):
         return total + rs2[k]
@@ -355,7 +359,7 @@
     t2[0] = DT * (1.2 * two_thirds(n * (1.0 / STATES)) - 1.0)
     t2[1] = kr * (-3.0 * DT / STATES)
     t2[2] = ki * (-3.0 * DT / STATES)
-    start(ag2_copy)
+    start(ag2_copy, groups)
     ag2[g] = t2[...]
 
     def kinetic_state(s, _):
@@ -378,7 +382,7 @@
         return 0
 
     lax.fori_loop(0, 4, kinetic_state, 0)
-    wait_recv(ag2, ag2_recv)
+    wait_recv(ag2, ag2_recv, groups, g)
 
     def correct(p, _):
         pot, dr, di = (jnp.concatenate([ag2[p, q], ag2[8 + p, q]], axis=0) for q in range(3))
@@ -398,10 +402,12 @@
 
     lax.fori_loop(0, 8, correct, 0)
 
-    for make in (rs1_copy, ag1_copy, rs2_copy, ag2_copy):
-        wait_send(make)
-    s1_copy(1).wait_send()
-    s1_copy(2).wait_send()
+    wait_send(rs1_copy, 8)
+    wait_send(ag1_copy, 8)
+    wait_send(rs2_copy, groups)
+    wait_send(ag2_copy, groups)
+    for case in cases:
+        s1_copy(*case).wait_send()
 
     def moves_sent(s, _):
         for c in range(2):
@@ -423,7 +429,7 @@
     out = pl.pallas_call(
         kernel,
         out_shape=jax.ShapeDtypeStruct((32, 64, 128), f32),
-        in_specs=[smem, smem, pl.BlockSpec(memory_space=pl.ANY)],
+        in_specs=[smem, smem, pl.BlockSpec(memory_space=pltpu.HBM)],
         out_specs=pl.BlockSpec(memory_space=pltpu.VMEM),
         scratch_shapes=[
             pltpu.VMEM((2, 4, 4, 8, 1024), f32),
@@ -432,12 +438,12 @@
             pltpu.VMEM((32, 112, 128), f32),
             pltpu.VMEM((32, 112, 128), f32),
             pltpu.VMEM((2, 14, 2, 8, 128), f32),
-            pltpu.VMEM((16, 3, 8, 128), f32),
-            pltpu.VMEM((16, 3, 8, 128), f32),
-            pltpu.VMEM((3, 8, 128), f32),
+            pltpu.VMEM((8, 2, 3, 8, 128), f32),
+            pltpu.VMEM((8, 2, 3, 8, 128), f32),
             pltpu.VMEM((2, 3, 8, 128), f32),
-            pltpu.VMEM((3, 8, 128), f32),
-            pltpu.VMEM((16, 3, 8, 128), f32),
+            pltpu.VMEM((2, 2, 2, 3, 8, 128), f32),
+            pltpu.VMEM((2, 3, 8, 128), f32),
+            pltpu.VMEM((8, 2, 3, 8, 128), f32),
             pltpu.VMEM((3, 8, 8, 128), f32),
             pltpu.VMEM((3, 8, 8, 128), f32),
             pltpu.VMEM((16, 3, 4, 128), f32),
@@ -445,7 +451,7 @@
             pltpu.VMEM((3, 4, 128), f32),
             pltpu.VMEM((16, 3, 4, 128), f32),
             dma((2,)), dma((3, 2, 4)), dma((3, 2, 4)),
-            dma((16,)), dma((16,)), dma((2,)), dma((2,)), dma((16,)), dma((16,)),
+            dma((8,)), dma((8,)), dma((2, 2, 2)), dma((2, 2, 2)), dma((8,)), dma((8,)),
             dma((16,)), dma((16,)), dma((16,)), dma((16,)), dma((2, 4)), dma((2, 4)),
         ],
         compiler_params=pltpu.CompilerParams(

time: 69.7 us -> 69.2 us (level)
  Pallas kernels: 67.2 us -> 65.5 us
  local copies, waits for them, and re-layouts: 2.31 us -> 3.51 us
    pallas_call x1, Pallas kernels: 67.2 us -> 65.5 us  [local(): pl.pallas_call(kernel, out_shape=jax.ShapeDtypeStruct((32, 64, 128), f32)...]
    unnamed x1 -> x7, local copies, waits for them, and re-layouts: 2.31 us -> 3.51 us
where the time goes in v3:
time: 69.2 us; the launch traced here: 69 us
  Pallas kernels  65.5 us (95%)
  local copies, waits for them, and re-layouts  3.51 us (5%)
    pallas_call x1, Pallas kernels, local(): pl.pallas_call(kernel, out_shape=jax.ShapeDtypeStruct((32, 64, 128), f32)...  65.5 us
    unnamed x7, local copies, waits for them, and re-layouts  3.51 us

profile of v3, /device:TPU:2, one launch (start us, length us, event | category | flops | bytes accessed | tf_op | source)
XLA Modules:
  0.0 69.0 jit_solution(17792919667872038302)
XLA Ops:
  0.0 0.0 copy-start
  0.0 1.2 %copy-done = f32[2,4,4,8,1024]{4,3,2,1,0:T(8,128)S(1)} copy-done((f32[2,4,4,8,1024]{4,3,2,1,0:T(8,128)S(1)}, f32[2,4,4,8,1024]{4,3,2,1,0:T(8,128)}, u32[]{:S(2)}) %copy-start) | copy-done | bytes 1048600
  1.2 0.0 copy-start.1
  1.2 0.7 copy-done.1
  1.9 0.0 copy-start.2
  1.9 0.7 copy-done.2
  2.5 65.5 %shard_map.37 = f32[32,64,128]{2,1,0:T(8,128)S(1)} custom-call(s32[2]{0:T(128)S(1)} %copy-done.1, s32[2]{0:T(128)S(1)} %copy-done.2, f32[2,4,4,8,1024]{4,3,2,1,0:T(8,128)S(1)} %copy-done), custom_call_target="tpu_custom_call" | custom-call | tf_op jit(solution)/shard_map/pallas_call | solution.py:429
  68.1 1.0 %copy.5 = f32[2,4,4,8,1024]{4,3,2,1,0:T(8,128)} copy(f32[2,4,4,8,1024]{4,3,2,1,0:T(8,128)S(1)} %bitcast.5) | data formatting | bytes 2097152
Async XLA Ops:
  0.0 1.2 %copy-start = (f32[2,4,4,8,1024]{4,3,2,1,0:T(8,128)S(1)}, f32[2,4,4,8,1024]{4,3,2,1,0:T(8,128)}, u32[]{:S(2)}) copy-start(f32[2,4,4,8,1024]{4,3,2,1,0:T(8,128)} %x_ref.1) | copy-start | bytes 3145732
  1.2 0.7 copy-start.1
  1.9 0.7 copy-start.2

commit v4 on v3

--- a/solution.py
+++ b/solution.py
@@ -10,10 +10,11 @@
 MESH = pl.DeviceIdType.MESH
 W = (-49.0 / 18.0, 1.5, -0.15, 1.0 / 90.0)
 DT = 0.1
+EARLY, SECOND = 1, 2
 VMEM_LIMIT = 44 * 2**20
 NZ = 128
 STATES = 64
-M = 4
+M = 8
 ONE, THREE, TWO = 0, 1, 2
 
 
@@ -57,9 +58,9 @@
     return y * y
 
 
-def kernel(shift_ref, boost_ref, x_ref, o_ref,
-           x_buf, land, e_buf, b_buf, p_buf, trig, d1, rs1, t1, s1, sel1, ag1, f0, acc, d2, rs2, t2, ag2,
-           x_sem, slab_send, slab_recv, rs1_send, rs1_recv, s1_send, s1_recv, ag1_send, ag1_recv,
+def kernel(shift_in, boost_in, x_ref, o_ref,
+           shift_ref, boost_ref, x_buf, land, e_buf, b_buf, p_buf, trig, d1, rs1, t1, swapped, s1, sel1, ag1, f0, acc, d2, rs2, t2, ag2,
+           x_sem, slab_send, slab_recv, rs1_send, rs1_recv, swap_sem, s1_send, s1_recv, ag1_send, ag1_recv,
            rs2_send, rs2_recv, ag2_send, ag2_recv, halo_send, halo_recv):
     slabs = lax.axis_size("slab")
     groups = lax.axis_size("grp")
@@ -79,12 +80,13 @@
 
     own_copy(0).start()
     own_copy(1).start()
+    given = [pltpu.make_async_copy(a, b, x_sem.at[2 + n]) for n, (a, b) in enumerate(((shift_in, shift_ref), (boost_in, boost_ref)))]
+    for copy in given:
+        copy.start()
 
     barrier = pltpu.get_barrier_semaphore()
     for d in (1, -1, 2, -2, 3, -3):
         pl.semaphore_signal(barrier, inc=1, device_id=slab(d), device_id_type=MESH)
-    for d in (1, -1, 2, -2):
-        pl.semaphore_signal(barrier, inc=1, device_id=(slab(d)[0], lax.rem(g + 8, groups)), device_id_type=MESH)
 
     def greet(k, _):
         pl.semaphore_signal(barrier, inc=1, device_id=peer(k), device_id_type=MESH)
@@ -119,6 +121,9 @@
 
         lax.fori_loop(0, 8, terms, 0)
 
+    for copy in given:
+        copy.wait()
+
     def phases(m, _):
         c = m // 14
         q = lax.rem(m, 14)
@@ -131,7 +136,7 @@
     lax.fori_loop(0, 28, phases, 0)
     acc[...] = jnp.zeros_like(acc)
 
-    pl.semaphore_wait(barrier, 10 + groups - 1)
+    pl.semaphore_wait(barrier, 6 + groups - 1)
 
     column = g // 8
     z_own = lax.rem(g, 8)
@@ -143,10 +148,8 @@
         return column * 8 + lax.rem(z_own + k, 8)
 
     def start(make, count):
-        def body(k, _):
+        for k in sorted(range(1, count), key=lambda k: -min(k % 8, 8 - k % 8)):
             make(k).start()
-            return 0
-        lax.fori_loop(1, count, body, 0)
 
     def wait_send(make, count):
         def body(k, _):
@@ -217,7 +220,7 @@
         forward_three(s).start()
 
     start(rs1_copy, 8)
-    lax.fori_loop(0, 4, start_moves, 0)
+    lax.fori_loop(0, EARLY, start_moves, 0)
     rs1[z_own] = d1[z_own]
 
     wait_recv(rs1, rs1_recv, 8, z_own)
@@ -226,24 +229,32 @@
         return total + rs1[k]
 
     t1[...] = lax.fori_loop(1, 8, add1, rs1[0])
-
-    def s1_copy(c, d, x):
+    swap = pltpu.make_async_remote_copy(
+        src_ref=t1, dst_ref=swapped, send_sem=swap_sem.at[0], recv_sem=swap_sem.at[1],
+        device_id=peer(8), device_id_type=MESH)
+    swap.start()
+    lax.fori_loop(EARLY, SECOND, start_moves, 0)
+    swap.wait()
+    t1[...] += swapped[...]
+
+    def s1_copy(c, d):
         return pltpu.make_async_remote_copy(
-            src_ref=t1.at[c], dst_ref=s1.at[c, d, column], send_sem=s1_send.at[c, d, x], recv_sem=s1_recv.at[c, d, column],
-            device_id=(slab((1 - 2 * c) * (d + 1))[0], x * 8 + z_own), device_id_type=MESH)
-
-    cases = [(c, d, x) for c in range(2) for d in range(2) for x in range(2)]
+            src_ref=t1.at[c], dst_ref=s1.at[c, d], send_sem=s1_send.at[c, d], recv_sem=s1_recv.at[c, d],
+            device_id=slab((1 - 2 * c) * (d + 1)), device_id_type=MESH)
+
+    cases = [(c, d) for c in range(2) for d in range(2)]
     for case in cases:
         s1_copy(*case).start()
+    lax.fori_loop(SECOND, 4, start_moves, 0)
     forward(0)
-    for c, d, x in cases:
-        pltpu.make_async_copy(s1.at[c, d, x], s1.at[c, d, x], s1_recv.at[c, d, x]).wait()
+    for case in cases:
+        s1_copy(*case).wait_recv()
     r0 = shift_ref[0] - 8
     r1 = shift_ref[1] - 8
     from_0 = ((z_own + r0) >> 3) & 1
     from_1 = ((7 - z_own + r1) >> 3) & 1
-    sel1[0] = s1[0, from_0, 0] + s1[0, from_0, 1]
-    sel1[1] = s1[1, from_1, 0] + s1[1, from_1, 1]
+    sel1[0] = s1[0, from_0]
+    sel1[1] = s1[1, from_1]
     start(ag1_copy, 8)
     ag1[z_own] = sel1[...]
     forward(1)
@@ -424,14 +435,17 @@
 
 def local(cloud_states, cloud_shift, boost_wave):
     f32 = jnp.float32
-    smem = pl.BlockSpec(memory_space=pltpu.SMEM)
+    hbm = pl.BlockSpec(memory_space=pltpu.HBM)
+    operands = [pltpu.with_memory_space_constraint(a, pltpu.HBM) for a in (cloud_shift, boost_wave, cloud_states)]
     dma = pltpu.SemaphoreType.DMA
     out = pl.pallas_call(
         kernel,
         out_shape=jax.ShapeDtypeStruct((32, 64, 128), f32),
-        in_specs=[smem, smem, pl.BlockSpec(memory_space=pltpu.HBM)],
+        in_specs=[hbm, hbm, hbm],
         out_specs=pl.BlockSpec(memory_space=pltpu.VMEM),
         scratch_shapes=[
+            pltpu.SMEM((2,), jnp.int32),
+            pltpu.SMEM((2,), jnp.int32),
             pltpu.VMEM((2, 4, 4, 8, 1024), f32),
             pltpu.VMEM((2, 4, 4, 256, 128), f32),
             pltpu.VMEM((4, 20, 8, 128), f32),
@@ -441,7 +455,8 @@
             pltpu.VMEM((8, 2, 3, 8, 128), f32),
             pltpu.VMEM((8, 2, 3, 8, 128), f32),
             pltpu.VMEM((2, 3, 8, 128), f32),
-            pltpu.VMEM((2, 2, 2, 3, 8, 128), f32),
+            pltpu.VMEM((2, 3, 8, 128), f32),
+            pltpu.VMEM((2, 2, 3, 8, 128), f32),
             pltpu.VMEM((2, 3, 8, 128), f32),
             pltpu.VMEM((8, 2, 3, 8, 128), f32),
             pltpu.VMEM((3, 8, 8, 128), f32),
@@ -450,13 +465,13 @@
             pltpu.VMEM((16, 3, 4, 128), f32),
             pltpu.VMEM((3, 4, 128), f32),
             pltpu.VMEM((16, 3, 4, 128), f32),
-            dma((2,)), dma((3, 2, 4)), dma((3, 2, 4)),
-            dma((8,)), dma((8,)), dma((2, 2, 2)), dma((2, 2, 2)), dma((8,)), dma((8,)),
+            dma((4,)), dma((3, 2, 4)), dma((3, 2, 4)),
+            dma((8,)), dma((8,)), dma((2,)), dma((2, 2)), dma((2, 2)), dma((8,)), dma((8,)),
             dma((16,)), dma((16,)), dma((16,)), dma((16,)), dma((2, 4)), dma((2, 4)),
         ],
         compiler_params=pltpu.CompilerParams(
             collective_id=0, has_side_effects=True, vmem_limit_bytes=VMEM_LIMIT),
-    )(cloud_shift, boost_wave, cloud_states)
+    )(*operands)
     out = out.reshape(2, 4, 4, 8, 8, 128).transpose(0, 1, 2, 4, 3, 5)
     return out.reshape(2, 4, 4, 8, 1024)
 

time: 69.2 us -> 53.4 us (0.77)
  Pallas kernels: 65.5 us -> 51.7 us
  local copies, waits for them, and re-layouts: 3.51 us -> 0.97 us
    pallas_call x1, Pallas kernels: 65.5 us -> 51.7 us  [local(): pl.pallas_call(kernel, out_shape=jax.ShapeDtypeStruct((32, 64, 128), f32)...]
    unnamed x7 -> x1, local copies, waits for them, and re-layouts: 3.51 us -> 0.97 us
where the time goes in v4:
time: 53.4 us; the launch traced here: 52.7 us
  Pallas kernels  51.7 us (97%)
  local copies, waits for them, and re-layouts  0.97 us (2%)
    pallas_call x1, Pallas kernels, local(): pl.pallas_call(kernel, out_shape=jax.ShapeDtypeStruct((32, 64, 128), f32)...  51.7 us

profile of v4, /device:TPU:2, one launch (start us, length us, event | category | flops | bytes accessed | tf_op | source)
XLA Modules:
  0.0 52.7 jit_solution(16709852562661341145)
XLA Ops:
  0.0 51.7 %shard_map.37 = f32[32,64,128]{2,1,0:T(8,128)S(1)} custom-call(s32[2]{0:T(128)} %shift_in.1, s32[2]{0:T(128)} %boost_in.1, f32[2,4,4,8,1024]{4,3,2,1,0:T(8,128)} %x_ref.1), custom_call_target="tpu_custom_call" | custom-call | tf_op jit(solution)/shard_map/pallas_call | solution.py:441
  51.7 1.0 %copy.5 = f32[2,4,4,8,1024]{4,3,2,1,0:T(8,128)} copy(f32[2,4,4,8,1024]{4,3,2,1,0:T(8,128)S(1)} %bitcast.5) | data formatting | bytes 2097152

commit v5 on v4

--- a/solution.py
+++ b/solution.py
@@ -15,7 +15,7 @@
 NZ = 128
 STATES = 64
 M = 8
-ONE, THREE, TWO = 0, 1, 2
+ONE, THREE, TWO, EDGE, REST = range(5)
 
 
 def stencil_tables(scale):
@@ -190,6 +190,12 @@
     def far_copy(c, s):
         return move(TWO, c, s, 24 - 24 * c, 8 + 8 * c, 8, slab(2 - 4 * c))
 
+    def last_copies():
+        to = slab(2 - 4 * core), slab(4 * core - 2)
+        return (move(TWO, 1 - core, 3, 24 * core, 16 - 8 * core, 8, to[1]),
+                move(EDGE, core, 3, 30 - 30 * core, 14 + 2 * core, 2, to[0]),
+                move(REST, core, 3, 24 - 22 * core, 8 + 10 * core, 6, to[0]))
+
     def near_copy(s):
         return move(ONE, core, s, 24 - 24 * core, 16 - 8 * core, 8, (mate, g))
 
@@ -206,12 +212,11 @@
         here = window(c, s, 0, planes)
         pltpu.make_async_copy(here, here, slab_recv.at[slot, c, s]).wait()
 
-    def start_moves(s, _):
-        far_copy(0, s).start()
-        far_copy(1, s).start()
+    def start_moves(s):
+        for copy in last_copies() if s == 3 else (far_copy(0, s), far_copy(1, s)):
+            copy.start()
         near_copy(s).start()
         third_copy(s).start()
-        return 0
 
     def forward(s):
         arrived(TWO, 0, s, 8)
@@ -219,8 +224,15 @@
         forward_one(s).start()
         forward_three(s).start()
 
+    def forward_last():
+        arrived(TWO, 1 - core, 3, 8)
+        forward_one(3).start()
+        arrived(EDGE, core, 3, 2)
+        forward_three(3).start()
+
     start(rs1_copy, 8)
-    lax.fori_loop(0, EARLY, start_moves, 0)
+    for s in range(EARLY):
+        start_moves(s)
     rs1[z_own] = d1[z_own]
 
     wait_recv(rs1, rs1_recv, 8, z_own)
@@ -233,7 +245,8 @@
         src_ref=t1, dst_ref=swapped, send_sem=swap_sem.at[0], recv_sem=swap_sem.at[1],
         device_id=peer(8), device_id_type=MESH)
     swap.start()
-    lax.fori_loop(EARLY, SECOND, start_moves, 0)
+    for s in range(EARLY, SECOND):
+        start_moves(s)
     swap.wait()
     t1[...] += swapped[...]
 
@@ -245,7 +258,8 @@
     cases = [(c, d) for c in range(2) for d in range(2)]
     for case in cases:
         s1_copy(*case).start()
-    lax.fori_loop(SECOND, 4, start_moves, 0)
+    for s in range(SECOND, 4):
+        start_moves(s)
     forward(0)
     for case in cases:
         s1_copy(*case).wait_recv()
@@ -335,18 +349,21 @@
 
             lax.fori_loop(0, 8 // M, predict, 0)
 
-        @pl.when(s < 2)
+        @pl.when(s == 0)
         def _():
-            forward(s + 2)
+            forward(2)
 
         @pl.when(s == 1)
         def _():
-            send_halos(0)
-            send_halos(1)
+            forward_last()
+
+        @pl.when(s < 3)
+        def _():
+            send_halos(s)
 
         @pl.when(s == 2)
         def _():
-            send_halos(2)
+            arrived(REST, core, 3, 6)
 
         return 0
 
@@ -422,7 +439,6 @@
 
     def moves_sent(s, _):
         for c in range(2):
-            far_copy(c, s).wait_send()
             halo_copy(c, s).wait_send()
         near_copy(s).wait_send()
         third_copy(s).wait_send()
@@ -431,6 +447,9 @@
         return 0
 
     lax.fori_loop(0, 4, moves_sent, 0)
+    for s in range(4):
+        for copy in last_copies() if s == 3 else (far_copy(0, s), far_copy(1, s)):
+            copy.wait_send()
 
 
 def local(cloud_states, cloud_shift, boost_wave):
@@ -465,7 +484,7 @@
             pltpu.VMEM((16, 3, 4, 128), f32),
             pltpu.VMEM((3, 4, 128), f32),
             pltpu.VMEM((16, 3, 4, 128), f32),
-            dma((4,)), dma((3, 2, 4)), dma((3, 2, 4)),
+            dma((4,)), dma((5, 2, 4)), dma((5, 2, 4)),
             dma((8,)), dma((8,)), dma((2,)), dma((2, 2)), dma((2, 2)), dma((8,)), dma((8,)),
             dma((16,)), dma((16,)), dma((16,)), dma((16,)), dma((2, 4)), dma((2, 4)),
         ],

time: 53.4 us -> 52.7 us (0.987)
  no operation moved by 1% of the time
where the time goes in v5:
time: 52.7 us; the launch traced here: 52.5 us
  Pallas kernels  51.5 us (98%)
  local copies, waits for them, and re-layouts  0.97 us (2%)
    pallas_call x1, Pallas kernels, local(): pl.pallas_call(kernel, out_shape=jax.ShapeDtypeStruct((32, 64, 128), f32)...  51.5 us

profile of v5, /device:TPU:2, one launch (start us, length us, event | category | flops | bytes accessed | tf_op | source)
XLA Modules:
  0.0 52.5 jit_solution(6741799997511366894)
XLA Ops:
  0.0 51.5 %shard_map.37 = f32[32,64,128]{2,1,0:T(8,128)S(1)} custom-call(s32[2]{0:T(128)} %shift_in.1, s32[2]{0:T(128)} %boost_in.1, f32[2,4,4,8,1024]{4,3,2,1,0:T(8,128)} %x_ref.1), custom_call_target="tpu_custom_call" | custom-call | tf_op jit(solution)/shard_map/pallas_call | solution.py:460
  51.5 1.0 %copy.5 = f32[2,4,4,8,1024]{4,3,2,1,0:T(8,128)} copy(f32[2,4,4,8,1024]{4,3,2,1,0:T(8,128)S(1)} %bitcast.5) | data formatting | bytes 2097152

commit v6 on v5

--- a/solution.py
+++ b/solution.py
@@ -59,7 +59,7 @@
 
 
 def kernel(shift_in, boost_in, x_ref, o_ref,
-           shift_ref, boost_ref, x_buf, land, e_buf, b_buf, p_buf, trig, d1, rs1, t1, swapped, s1, sel1, ag1, f0, acc, d2, rs2, t2, ag2,
+           shift_ref, boost_ref, x_buf, land, e_buf, b_buf, p_buf, h_buf, trig, d1, rs1, t1, swapped, s1, sel1, ag1, f0, acc, d2, rs2, t2, ag2,
            x_sem, slab_send, slab_recv, rs1_send, rs1_recv, swap_sem, s1_send, s1_recv, ag1_send, ag1_recv,
            rs2_send, rs2_recv, ag2_send, ag2_recv, halo_send, halo_recv):
     slabs = lax.axis_size("slab")
@@ -135,6 +135,8 @@
 
     lax.fori_loop(0, 28, phases, 0)
     acc[...] = jnp.zeros_like(acc)
+    p_buf[:, 0:24, :] = jnp.zeros((32, 24, 128), jnp.float32)
+    p_buf[:, 88:112, :] = jnp.zeros((32, 24, 128), jnp.float32)
 
     pl.semaphore_wait(barrier, 6 + groups - 1)
 
@@ -294,10 +296,10 @@
 
     def halo_copy(d, s):
         src = pl.ds(24, 24) if d == 0 else pl.ds(64, 24)
-        dst = pl.ds(88, 24) if d == 0 else pl.ds(0, 24)
+        dst = pl.ds(24, 24) if d == 0 else pl.ds(0, 24)
         vols = pl.ds(s * 8, 8)
         return pltpu.make_async_remote_copy(
-            src_ref=p_buf.at[vols, src], dst_ref=p_buf.at[vols, dst],
+            src_ref=p_buf.at[vols, src], dst_ref=h_buf.at[vols, dst],
             send_sem=halo_send.at[d, s], recv_sem=halo_recv.at[d, s],
             device_id=slab(2 * d - 1), device_id_type=MESH)
 
@@ -377,23 +379,7 @@
 
     start(rs2_copy, groups)
     send_halos(3)
-    rs2[g] = d2[g]
-    wait_recv(rs2, rs2_recv, groups, g)
-
-    def add2(k, total):
-        return total + rs2[k]
-
-    n, kr, ki = lax.fori_loop(1, groups, add2, rs2[0])
-    t2[0] = DT * (1.2 * two_thirds(n * (1.0 / STATES)) - 1.0)
-    t2[1] = kr * (-3.0 * DT / STATES)
-    t2[2] = ki * (-3.0 * DT / STATES)
-    start(ag2_copy, groups)
-    ag2[g] = t2[...]
-
     def kinetic_state(s, _):
-        halo_copy(0, s).wait_recv()
-        halo_copy(1, s).wait_recv()
-
         def kinetic(m, _):
             vol = (s * 2 + m // (8 // M)) * 4
             row = pl.multiple_of((lax.rem(m, 8 // M) * M + 3) * 8, 8)
@@ -409,10 +395,49 @@
         lax.fori_loop(0, 16 // M, kinetic, 0)
         return 0
 
-    lax.fori_loop(0, 4, kinetic_state, 0)
-    wait_recv(ag2, ag2_recv, groups, g)
-
-    def correct(p, _):
+    def edge_state(s, _):
+        halo_copy(0, s).wait_recv()
+        halo_copy(1, s).wait_recv()
+        w1, w2, w3 = tables[0][1:]
+
+        def edges(c, _):
+            vol = (s * 2 + c) * 4
+            for k, other, sign in ((0, 1, -1.0), (1, 0, 1.0), (2, 3, 1.0), (3, 2, -1.0)):
+                for near, far in (((16, 8, 0), (24, 32, 40)), ((24, 32, 40), (80, 72, 64))):
+                    h1, h2, h3 = (sign * h_buf[vol + other, row:row + 8, :] for row in near)
+                    for row, v in zip(far, (w1 * h1 + w2 * h2 + w3 * h3, w2 * h1 + w3 * h2, w3 * h1)):
+                        b_buf[vol + k, row:row + 8, :] += v
+            return 0
+
+        lax.fori_loop(0, 2, edges, 0)
+        return 0
+
+    rs2[g] = d2[g]
+    lax.fori_loop(0, 3, kinetic_state, 0)
+    wait_recv(rs2, rs2_recv, groups, g)
+
+    def add2(k, total):
+        return total + rs2[k]
+
+    n, kr, ki = lax.fori_loop(1, groups, add2, rs2[0])
+    t2[0] = DT * (1.2 * two_thirds(n * (1.0 / STATES)) - 1.0)
+    t2[1] = kr * (-3.0 * DT / STATES)
+    t2[2] = ki * (-3.0 * DT / STATES)
+    start(ag2_copy, groups)
+    ag2[g] = t2[...]
+
+    lax.fori_loop(3, 4, kinetic_state, 0)
+    lax.fori_loop(0, 4, edge_state, 0)
+
+    def correct(t, _):
+        p = (z_own + (1 - 2 * lax.rem(t, 2)) * ((t + 1) // 2) + 8) & 7
+        for half in range(2):
+            o = 8 * half + p
+
+            @pl.when(o != g)
+            def _():
+                pltpu.make_async_copy(ag2.at[o], ag2.at[o], ag2_recv.at[o]).wait()
+
         pot, dr, di = (jnp.concatenate([ag2[p, q], ag2[8 + p, q]], axis=0) for q in range(3))
         at = pl.ds(pl.multiple_of((p + 3) * 8, 8), 8)
         to = pl.ds(p, 8, stride=8)
@@ -470,6 +495,7 @@
             pltpu.VMEM((4, 20, 8, 128), f32),
             pltpu.VMEM((32, 112, 128), f32),
             pltpu.VMEM((32, 112, 128), f32),
+            pltpu.VMEM((32, 48, 128), f32),
             pltpu.VMEM((2, 14, 2, 8, 128), f32),
             pltpu.VMEM((8, 2, 3, 8, 128), f32),
             pltpu.VMEM((8, 2, 3, 8, 128), f32),

time: 52.7 us -> 52.1 us (0.989)
  no operation moved by 1% of the time
where the time goes in v6:
time: 52.1 us; the launch traced here: 52 us
  Pallas kernels  51 us (98%)
  local copies, waits for them, and re-layouts  0.97 us (2%)
    pallas_call x1, Pallas kernels, local(): pl.pallas_call(kernel, out_shape=jax.ShapeDtypeStruct((32, 64, 128), f32)...  51 us

profile of v6, /device:TPU:2, one launch (start us, length us, event | category | flops | bytes accessed | tf_op | source)
XLA Modules:
  0.0 52.0 jit_solution(14449917129337039695)
XLA Ops:
  0.0 51.0 %shard_map.37 = f32[32,64,128]{2,1,0:T(8,128)S(1)} custom-call(s32[2]{0:T(128)} %shift_in.1, s32[2]{0:T(128)} %boost_in.1, f32[2,4,4,8,1024]{4,3,2,1,0:T(8,128)} %x_ref.1), custom_call_target="tpu_custom_call" | custom-call | tf_op jit(solution)/shard_map/pallas_call | solution.py:485
  51.0 1.0 %copy.5 = f32[2,4,4,8,1024]{4,3,2,1,0:T(8,128)} copy(f32[2,4,4,8,1024]{4,3,2,1,0:T(8,128)S(1)} %bitcast.5) | data formatting | bytes 2097152

commit v7 on v6

--- a/solution.py
+++ b/solution.py
@@ -121,23 +121,6 @@
 
         lax.fori_loop(0, 8, terms, 0)
 
-    for copy in given:
-        copy.wait()
-
-    def phases(m, _):
-        c = m // 14
-        q = lax.rem(m, 14)
-        index = (boost_ref[c] * (8 * i + q - 3)) & (NZ - 1)
-        angle = jnp.full((8, 128), index, jnp.int32).astype(jnp.float32) * (2.0 * math.pi / NZ)
-        trig[c, q, 0] = jnp.cos(angle)
-        trig[c, q, 1] = jnp.sin(angle)
-        return 0
-
-    lax.fori_loop(0, 28, phases, 0)
-    acc[...] = jnp.zeros_like(acc)
-    p_buf[:, 0:24, :] = jnp.zeros((32, 24, 128), jnp.float32)
-    p_buf[:, 88:112, :] = jnp.zeros((32, 24, 128), jnp.float32)
-
     pl.semaphore_wait(barrier, 6 + groups - 1)
 
     column = g // 8
@@ -160,11 +143,9 @@
         lax.fori_loop(1, count, body, 0)
 
     def wait_recv(buf, sem, count, mine):
-        def body(k, _):
+        for k in range(1, count):
             o = lax.rem(mine + k, count)
             pltpu.make_async_copy(buf.at[o], buf.at[o], sem.at[o]).wait()
-            return 0
-        lax.fori_loop(1, count, body, 0)
 
     def exchange(src, dst, send, recv, one, count, mine):
         def make(k):
@@ -236,6 +217,23 @@
     for s in range(EARLY):
         start_moves(s)
     rs1[z_own] = d1[z_own]
+
+    for copy in given:
+        copy.wait()
+
+    def phases(m, _):
+        c = m // 14
+        q = lax.rem(m, 14)
+        index = (boost_ref[c] * (8 * i + q - 3)) & (NZ - 1)
+        angle = jnp.full((8, 128), index, jnp.int32).astype(jnp.float32) * (2.0 * math.pi / NZ)
+        trig[c, q, 0] = jnp.cos(angle)
+        trig[c, q, 1] = jnp.sin(angle)
+        return 0
+
+    lax.fori_loop(0, 28, phases, 0)
+    acc[...] = jnp.zeros_like(acc)
+    p_buf[:, 0:24, :] = jnp.zeros((32, 24, 128), jnp.float32)
+    p_buf[:, 88:112, :] = jnp.zeros((32, 24, 128), jnp.float32)
 
     wait_recv(rs1, rs1_recv, 8, z_own)
 
@@ -359,7 +357,7 @@
         def _():
             forward_last()
 
-        @pl.when(s < 3)
+        @pl.when(s < 2)
         def _():
             send_halos(s)
 
@@ -378,6 +376,7 @@
             d2[8 + p, q] = v[4:8]
 
     start(rs2_copy, groups)
+    send_halos(2)
     send_halos(3)
     def kinetic_state(s, _):
         def kinetic(m, _):

time: 52.1 us -> 52.4 us (level)
  no operation moved by 1% of the time
where the time goes in v7:
time: 52.4 us; the launch traced here: 52.3 us
  Pallas kernels  51.4 us (98%)
  local copies, waits for them, and re-layouts  0.97 us (2%)
    pallas_call x1, Pallas kernels, local(): pl.pallas_call(kernel, out_shape=jax.ShapeDtypeStruct((32, 64, 128), f32)...  51.4 us

profile of v7, /device:TPU:2, one launch (start us, length us, event | category | flops | bytes accessed | tf_op | source)
XLA Modules:
  0.0 52.3 jit_solution(10104795388946705030)
XLA Ops:
  0.0 51.4 %shard_map.37 = f32[32,64,128]{2,1,0:T(8,128)S(1)} custom-call(s32[2]{0:T(128)} %shift_in.1, s32[2]{0:T(128)} %boost_in.1, f32[2,4,4,8,1024]{4,3,2,1,0:T(8,128)} %x_ref.1), custom_call_target="tpu_custom_call" | custom-call | tf_op jit(solution)/shard_map/pallas_call | solution.py:484
  51.4 1.0 %copy.5 = f32[2,4,4,8,1024]{4,3,2,1,0:T(8,128)} copy(f32[2,4,4,8,1024]{4,3,2,1,0:T(8,128)S(1)} %bitcast.5) | data formatting | bytes 2097152
